TPU v7x, 256 devices: a whole 4x4x8 slice. The times are simulated.
256 devices in a mesh: crop: 2 (over core), row: 8 (over x_hi, y), col: 16 (over z, x_lo).
Axes of the slice: x: 4 (x_hi: 2, x_lo: 2; x = x_hi * 2 + x_lo), y: 4, z: 8, core: 2. Of those that a mesh axis runs over, the one named last changes fastest.
Arguments:
- pair_state: bfloat16 [768, 384, 128], P(('crop', 'row'), 'col'), parts along dimension 0, may hold values from -6 to 6
- token_mask: int32 [768], P('crop'), parts along dimension 0, may hold values from 0 to 1, as said below
- block_pattern: int32 [8, 4], P('crop'), parts along dimension 0, may hold values from 0 to 1, as said below
- triangle_norm: float32 [128], replicated, may hold values from 0.1 to 1.9
- triangle_input: bfloat16 [128, 512], replicated, may hold values from -0.5 to 0.5
- triangle_gate: bfloat16 [128, 128], replicated, may hold values from -0.5 to 0.5
- product_norm: float32 [128], replicated, may hold values from 0.1 to 1.9
- triangle_output: bfloat16 [128, 128], replicated, may hold values from -0.5 to 0.5
- attend_norm: float32 [128], replicated, may hold values from 0.1 to 1.9
- attend_inputs: bfloat16 [128, 384], replicated, may hold values from -4 to 4
- attend_gate: bfloat16 [128, 128], replicated, may hold values from -0.5 to 0.5
- attend_bias: bfloat16 [128, 4], replicated, may hold values from -0.5 to 0.5
- attend_output: bfloat16 [128, 128], replicated, may hold values from -0.5 to 0.5
Outputs:
- pair_output: bfloat16 [768, 384, 128], P(('crop', 'row'), 'col'), parts along dimension 0
There are 2 independent parts, one for each index of `crop`. A program takes and returns all parts, laid end to end along the dimension named above; an argument that names none is the same for every part. Nothing has to cross between parts.
Inputs may be any that keep to these rules, and one draw needn't show every extreme that they name: `token_mask`: 1 on a prefix of 96 or more tokens and 0 after it. `block_pattern`: every row allows its own block and block 0.
All inputs are finite; a program needn't handle non-finite values.
Results may differ from a plain program's by a relative error of at most 0.02.
Values may be sent and summed in bfloat16 or wider, within the bound.
A program may use at most 64 MiB of HBM per device.

v0:
```python
import math

import jax
import jax.numpy as jnp
from jax import lax
from jax.sharding import Mesh
from jax.sharding import PartitionSpec as P

ROW = ("row_0", "row_1")
COL = ("col_0", "col_1")
ROW_COL = ("row_0", "row_1", "col_0", "col_1")
CROP_ROW = ("crop", "row_0", "row_1")


norm_epsilon = 1e-05


def joined_along(pieces, dim):
    lengths = list(pieces.shape[1:])
    lengths[dim] *= pieces.shape[0]
    return jnp.moveaxis(pieces, 0, dim).reshape(lengths)


def gather_in_order(array, axes, turns):
    pieces = array[None]
    for k in turns:
        pieces = lax.all_gather(pieces, axes[k], axis=0, tiled=True)
    held = [lax.axis_size(axes[k]) for k in reversed(turns)]
    pieces = pieces.reshape(*held, *array.shape)
    turned = sorted(range(len(turns)), key=lambda place: turns[len(turns) - 1 - place])
    return pieces.transpose(*turned, *range(len(turns), pieces.ndim)).reshape(-1, *array.shape)


def whole_of(array, axes, turns, dim):
    return joined_along(gather_in_order(array, axes, turns), dim)


def layer_norm(inputs, gain):
    average = jnp.mean(inputs, axis=-1, keepdims=True)
    centered = inputs - average
    variance = jnp.mean(centered * centered, axis=-1, keepdims=True)
    return centered * lax.rsqrt(variance + norm_epsilon) * gain


def project_rows(pair_rows, attend_inputs, attend_gate, head_count):
    row_count, token_count, channels = pair_rows.shape
    head_width = channels // head_count
    combined = jnp.dot(pair_rows, attend_inputs, preferred_element_type=jnp.float32)
    queries = (
        combined[..., :channels]
        .astype(jnp.bfloat16)
        .reshape(row_count, token_count, head_count, head_width)
    )
    key_rows = (
        combined[..., channels : 2 * channels]
        .astype(jnp.bfloat16)
        .reshape(row_count, token_count, head_count, head_width)
    )
    values = (
        combined[..., 2 * channels :]
        .astype(jnp.bfloat16)
        .reshape(row_count, token_count, head_count, head_width)
    )
    gate_values = jax.nn.sigmoid(
        jnp.dot(pair_rows, attend_gate, preferred_element_type=jnp.float32)
    )
    return (queries, key_rows, values, gate_values)


def attend_dense(pair_rows, attend_inputs, attend_gate, head_bias, allowed):
    row_count, token_count, channels = pair_rows.shape
    head_count = head_bias.shape[0]
    queries, key_rows, values, gate_values = project_rows(
        pair_rows, attend_inputs, attend_gate, head_count
    )
    scores = jnp.einsum(
        "rjhd,rkhd->rhjk", queries, key_rows, preferred_element_type=jnp.float32
    ) / math.sqrt(channels // head_count)
    scores = scores + head_bias.astype(jnp.float32)[None]
    scores = jnp.where(allowed[None, None], scores, -jnp.inf)
    row_max = jnp.max(scores, axis=-1, keepdims=True)
    weights = jnp.exp(scores - row_max)
    probabilities = (weights / jnp.sum(weights, axis=-1, keepdims=True)).astype(jnp.bfloat16)
    attended = jnp.einsum(
        "rhjk,rkhd->rjhd", probabilities, values, preferred_element_type=jnp.float32
    ).reshape(row_count, token_count, channels)
    return (gate_values * attended).astype(jnp.bfloat16)


def shards(
    pair_state,
    token_mask,
    block_pattern,
    triangle_norm,
    triangle_input,
    triangle_gate,
    product_norm,
    triangle_output,
    attend_norm,
    attend_inputs,
    attend_gate,
    attend_bias,
    attend_output,
):
    tile_rows, tile_columns, channels = pair_state.shape
    row_devices = lax.axis_size(ROW)
    column_devices = lax.axis_size(COL)
    token_count = tile_columns * column_devices
    row_index = lax.axis_index(ROW)
    column_index = lax.axis_index(COL)
    valid_tokens = token_mask.astype(jnp.float32)
    row_valid = lax.dynamic_slice_in_dim(valid_tokens, row_index * tile_rows, tile_rows)
    column_valid = lax.dynamic_slice_in_dim(valid_tokens, column_index * tile_columns, tile_columns)
    state_float = pair_state.astype(jnp.float32)
    normed = layer_norm(state_float, triangle_norm).astype(jnp.bfloat16)
    projected = jnp.dot(normed, triangle_input, preferred_element_type=jnp.float32)
    pair_valid = (row_valid[:, None] * column_valid[None, :])[:, :, None]
    left_factor = (
        pair_valid
        * jax.nn.sigmoid(projected[..., :channels])
        * projected[..., channels : 2 * channels]
    ).astype(jnp.bfloat16)
    right_factor = (
        pair_valid
        * jax.nn.sigmoid(projected[..., 2 * channels : 3 * channels])
        * projected[..., 3 * channels :]
    ).astype(jnp.bfloat16)
    right_columns = lax.all_gather(right_factor, ROW, axis=0, tiled=True)
    summed_part = lax.dot_general(
        right_columns, left_factor, (((1,), (1,)), ((2,), (2,))), preferred_element_type=jnp.float32
    )
    flipped = lax.psum_scatter(
        jnp.transpose(summed_part, (1, 2, 0)), COL, scatter_dimension=0, tiled=True
    )
    product = jnp.transpose(flipped, (1, 0, 2))
    product_normed = layer_norm(product, product_norm).astype(jnp.bfloat16)
    gate_values = jax.nn.sigmoid(jnp.dot(normed, triangle_gate, preferred_element_type=jnp.float32))
    middle = (
        state_float
        + gate_values * jnp.dot(product_normed, triangle_output, preferred_element_type=jnp.float32)
    ).astype(jnp.bfloat16)
    attend_normed = layer_norm(middle.astype(jnp.float32), attend_norm).astype(jnp.bfloat16)
    head_count = attend_bias.shape[1]
    bias_tile = jnp.dot(attend_normed, attend_bias, preferred_element_type=jnp.float32).astype(
        jnp.bfloat16
    )
    flat_bias = jnp.transpose(bias_tile, (2, 0, 1)).reshape(head_count, tile_rows * tile_columns)
    gathered = whole_of(flat_bias, ROW_COL, (0, 3, 1, 2), 1)
    head_bias = gathered.reshape(head_count, row_devices, column_devices, tile_rows, tile_columns)
    head_bias = jnp.transpose(head_bias, (0, 1, 3, 2, 4)).reshape(
        head_count, token_count, token_count
    )
    blocks = block_pattern.shape[0]
    block_width = token_count // blocks
    pattern_ok = block_pattern[:, None, :, None] > 0
    allowed = jnp.broadcast_to(pattern_ok, (blocks, block_width, blocks, block_width)).reshape(
        token_count, token_count
    ) & (token_mask[None, :] > 0)
    rows_each = tile_rows // column_devices
    grouped = attend_normed.reshape(column_devices, rows_each, tile_columns, channels)
    received = lax.all_to_all(grouped, COL, split_axis=0, concat_axis=2, tiled=True)
    outer, inner, tokens_here, width_here = received.shape
    flat = received.reshape(outer * inner, tokens_here, width_here)
    attended_rows = attend_dense(flat, attend_inputs, attend_gate, head_bias, allowed).reshape(
        outer, inner, tokens_here, width_here
    )
    returned = lax.all_to_all(attended_rows, COL, split_axis=2, concat_axis=0, tiled=True)
    returned = returned.reshape(tile_rows, tile_columns, channels)
    update = jnp.dot(returned, attend_output, preferred_element_type=jnp.float32)
    return (middle.astype(jnp.float32) + update).astype(jnp.bfloat16)


def solution(mesh):
    finer = Mesh(
        mesh.devices.reshape(mesh.shape["crop"], 2, 4, 8, 2),
        ("crop", "row_0", "row_1", "col_0", "col_1"),
    )
    return jax.shard_map(
        shards,
        mesh=finer,
        in_specs=(
            P(CROP_ROW, COL, None),
            P("crop"),
            P("crop", None),
            P(),
            P(),
            P(),
            P(),
            P(),
            P(),
            P(),
            P(),
            P(),
            P(),
        ),
        out_specs=P(CROP_ROW, COL, None),
        check_vma=False,
    )
```

profile of v0, /device:TPU:2, one launch (start us, length us, event | category | flops | bytes accessed | tf_op | source)
XLA Modules:
  0.0 430.1 jit_solution(2989985232182543160)
XLA Ops:
  8.6 1.4 fusion.25
  10.1 1.5 fusion.39
  13.2 62.3 %all-gather.3.cloned.1.call-done = bf16[384,24,128]{2,1,0:T(8,128)(2,1)} async-done(((bf16[48,24,128]{2,1,0:T(8,128)(2,1)}), bf16[384,24,128]{2,1,0:T(8,128)(2,1)}) %all-gather.3.cloned.1.call-update) | async-done | bytes 2359312 | tf_op jit(solution)/shard_map/all_gather | solution.py:128
  75.6 3.7 copy.84
  79.3 5.1 %convolution_bitcast_fusion = f32[384,48,128]{0,1,2:T(8,128)} fusion(bf16[384,24,128]{0,1,2:T(8,128)(2,1)S(1)} %copy.84, bf16[48,24,128]{0,1,2:T(8,128)(2,1)S(1)} %copy.85), kind=kOutput, calls=%fused_computation.10 | convolution fusion | flops 113246208 | bytes 12091392 | tf_op jit(solution)/shard_map/dot_general | solution.py:129
  84.3 9.8 %copy.86 = f32[384,48,128]{2,1,0:T(8,128)} copy(f32[384,48,128]{0,1,2:T(8,128)} %convolution_bitcast_fusion) | data formatting | bytes 18874368 | tf_op jit(solution)/shard_map/transpose | solution.py:133
  95.7 200.2 %reduce-scatter.2.cloned.1.call-done = f32[24,48,128]{2,1,0:T(8,128)} async-done(((f32[384,48,128]{2,1,0:T(8,128)}), f32[24,48,128]{2,1,0:T(8,128)}) %reduce-scatter.2.cloned.1.call-update) | async-done | bytes 589840 | tf_op jit(solution)/shard_map/reduce_scatter | solution.py:132
  295.9 1.3 bitcast_reduce_fusion
  297.3 1.5 multiply_reduce_fusion.1
  299.0 1.4 multiply_convert_fusion.1
  302.4 1.6 fusion.20
  304.1 5.9 %all_gather.16 = bf16[2,4,1152]{2,1,0:T(4,128)(2,1)S(1)} all-gather(bf16[1,4,1152]{2,1,0:T(4,128)(2,1)S(1)} %broadcast_in_dim_reshape.3), channel_id=1, replica_groups=mesh['crop'=2,'row_0'=2,'row_1'=4,'col_0'=8,'col_1'=2] {'row_0'}, dimensions={0}, use_global_device_ids=true | all-gather | bytes 27648 | tf_op jit(solution)/shard_map/all_gather | solution.py:27
  310.0 4.4 %all_gather.17 = bf16[4,4,1152]{2,1,0:T(4,128)(2,1)S(1)} all-gather(bf16[2,4,1152]{2,1,0:T(4,128)(2,1)S(1)} %all_gather.16), channel_id=1, replica_groups=mesh['crop'=2,'row_0'=2,'row_1'=4,'col_0'=8,'col_1'=2] {'col_1'}, dimensions={0}, use_global_device_ids=true | all-gather | bytes 55296 | tf_op jit(solution)/shard_map/all_gather | solution.py:27
  314.4 13.4 %all_gather.18 = bf16[16,4,1152]{2,1,0:T(4,128)(2,1)} all-gather(bf16[4,4,1152]{2,1,0:T(4,128)(2,1)S(1)} %all_gather.17), channel_id=1, replica_groups=mesh['crop'=2,'row_0'=2,'row_1'=4,'col_0'=8,'col_1'=2] {'row_1'}, dimensions={0}, use_global_device_ids=true | all-gather | bytes 184320 | tf_op jit(solution)/shard_map/all_gather | solution.py:27
  327.9 8.4 %all-to-all-start = ((bf16[16,3,24,128]{3,2,1,0:T(8,128)(2,1)}), bf16[16,3,24,128]{3,2,1,0:T(8,128)(2,1)S(1)}, u32[]{:S(2)}, u32[]{:S(2)}) async-start(bf16[16,3,24,128]{3,2,1,0:T(8,128)(2,1)} %bitcast.5), calls=%async_computation.1 | async-start | bytes 589824 | tf_op jit(solution)/shard_map/all_to_all | solution.py:161
  337.1 9.4 %all-to-all-done = bf16[16,3,24,128]{3,2,1,0:T(8,128)(2,1)S(1)} async-done(((bf16[16,3,24,128]{3,2,1,0:T(8,128)(2,1)}), bf16[16,3,24,128]{3,2,1,0:T(8,128)(2,1)S(1)}, u32[]{:S(2)}, u32[]{:S(2)}) %all-to-all-start) | async-done | bytes 294944 | tf_op jit(solution)/shard_map/all_to_all | solution.py:161
  347.8 20.3 %all-gather.5.cloned.1.call-done = bf16[128,4,1152]{2,1,0:T(4,128)(2,1)} async-done(((bf16[16,4,1152]{2,1,0:T(4,128)(2,1)}), bf16[128,4,1152]{2,1,0:T(4,128)(2,1)}) %all-gather.5.cloned.1.call-update) | async-done | bytes 1179664 | tf_op jit(solution)/shard_map/all_gather | solution.py:27
  368.1 1.7 copy.96
  370.0 9.5 %reshape.148 = f32[4,8,16,48,24]{4,3,2,1,0:T(8,128)} reshape(f32[4,128,1152]{2,1,0:T(8,128)S(1)} %copy.97) | data formatting | bytes 4718592 | tf_op jit(solution)/shard_map/convert_element_type | solution.py:79
  379.5 10.7 %copy.98 = f32[4,8,48,16,24]{2,1,4,3,0:T(8,128)} copy(f32[4,8,48,16,24]{4,2,3,1,0:T(8,128)} %bitcast.76) | data formatting | bytes 4718592 | tf_op jit(solution)/shard_map/convert_element_type | solution.py:79
  390.2 4.8 %reshape.147 = f32[4,384,384]{1,2,0:T(8,128)S(1)} reshape(f32[4,8,48,16,24]{2,1,4,3,0:T(8,128)} %copy.98) | data formatting | bytes 4718592 | tf_op jit(solution)/shard_map/convert_element_type | solution.py:79
  394.9 6.6 %fusion.53 = (f32[3,4,384]{2,1,0:T(4,128)S(1)}, f32[3,4,384,384]{2,3,1,0:T(8,128)}) fusion(f32[4,384,384]{1,2,0:T(8,128)S(1)} %reshape.147, pred[384,384]{0,1:T(8,128)(4,1)S(1)} %broadcast_and_fusion, bf16[3,384,4,32]{1,3,2,0:T(8,128)(2,1)} %bitcast.87, bf16[3,384,4,32]{1,3,2,0:T(8,128)(2,1)} %bitcast.86), kind=kOutput, calls=%fused_computation.82 | convolution fusion | flops 122093952 | bytes 10192896 | tf_op jit(solution)/shard_map/sub | solution.py:82
  401.5 3.8 fusion.6
  406.2 16.3 %all_to_all.30 = bf16[1,3,384,128]{3,1,0,2:T(4,128)(2,1)S(1)} all-to-all(bf16[1,3,384,128]{3,1,0,2:T(4,128)(2,1)S(1)} %copy.101), channel_id=1, replica_groups=mesh['crop'=2,'row_0'=2,'row_1'=4,'col_0'=8,'col_1'=2] {'col_0','col_1'}, dimensions={2} | all-to-all | bytes 589824 | tf_op jit(solution)/shard_map/all_to_all | solution.py:167
  (72 shorter events, 11.8 us)
Async XLA Ops:
  6.5 3.5 copy-start
  6.5 69.0 %all-gather.3.cloned.1.call-start = ((), (), s32[]{:S(2)}) async-start(), calls=%async_computation.3 | async-start | bytes 2654208 | tf_op jit(solution)/shard_map/all_gather | solution.py:128
  12.7 283.2 %reduce-scatter.2.cloned.1.call-start = ((), (), s32[]{:S(2)}) async-start(), calls=%async_computation.4 | async-start | bytes 10027008 | tf_op jit(solution)/shard_map/reduce_scatter | solution.py:132
  94.2 1.0 copy-start.2
  94.2 1.0 copy-start.9
  94.2 1.0 copy-start.12
  94.2 204.8 %copy-start.10 = (f32[128]{0:T(128)S(1)}, f32[128]{0:T(128)}, u32[]{:S(2)}) copy-start(f32[128]{0:T(128)} %param.19) | copy-start | bytes 1540
  94.2 206.3 %copy-start.4 = (bf16[128,128]{1,0:T(8,128)(2,1)S(1)}, bf16[128,128]{1,0:T(8,128)(2,1)}, u32[]{:S(2)}) copy-start(bf16[128,128]{1,0:T(8,128)(2,1)} %param.20) | copy-start | bytes 98308
  94.2 207.1 %copy-start.11 = (f32[128]{0:T(128)S(1)}, f32[128]{0:T(128)}, u32[]{:S(2)}) copy-start(f32[128]{0:T(128)} %param.21) | copy-start | bytes 1540
  94.2 208.2 %copy-start.8 = (bf16[128,4]{0,1:T(4,128)(2,1)S(1)}, bf16[128,4]{0,1:T(4,128)(2,1)}, u32[]{:S(2)}) copy-start(bf16[128,4]{0,1:T(4,128)(2,1)} %param.24) | copy-start | bytes 3076
  94.2 242.0 %copy-start.7 = (s32[4,4]{1,0:T(4,128)S(1)}, s32[4,4]{1,0:T(4,128)}, u32[]{:S(2)}) copy-start(s32[4,4]{1,0:T(4,128)} %param.15) | copy-start | bytes 196
  94.2 242.6 %copy-start.6 = (s32[384]{0:T(512)S(1)}, s32[384]{0:T(512)}, u32[]{:S(2)}) copy-start(s32[384]{0:T(512)} %param.14) | copy-start | bytes 4612
  94.3 252.2 %copy-start.3 = (bf16[128,384]{1,0:T(8,128)(2,1)S(1)}, bf16[128,384]{1,0:T(8,128)(2,1)}, u32[]{:S(2)}) copy-start(bf16[128,384]{1,0:T(8,128)(2,1)} %param.22) | copy-start | bytes 294916
  94.3 273.8 %all-gather.5.cloned.1.call-start = ((), (), s32[]{:S(2)}) async-start(), calls=%async_computation.5 | async-start | bytes 1327104 | tf_op jit(solution)/shard_map/all_gather | solution.py:27
  327.9 18.6 %all-to-all-start = ((bf16[16,3,24,128]{3,2,1,0:T(8,128)(2,1)}), bf16[16,3,24,128]{3,2,1,0:T(8,128)(2,1)S(1)}, u32[]{:S(2)}, u32[]{:S(2)}) async-start(bf16[16,3,24,128]{3,2,1,0:T(8,128)(2,1)} %bitcast.5), calls=%async_computation.1 | async-start | bytes 589824 | tf_op jit(solution)/shard_map/all_to_all | solution.py:161
  401.5 4.0 copy-start.13
  401.5 21.0 %copy-start.5 = (bf16[128,128]{1,0:T(8,128)(2,1)S(1)}, bf16[128,128]{1,0:T(8,128)(2,1)}, u32[]{:S(2)}) copy-start(bf16[128,128]{1,0:T(8,128)(2,1)} %param.25) | copy-start | bytes 98308
  401.5 22.0 %copy-start.1 = (bf16[128,512]{1,0:T(8,128)(2,1)S(1)}, bf16[128,512]{1,0:T(8,128)(2,1)}, u32[]{:S(2)}) copy-start(bf16[128,512]{1,0:T(8,128)(2,1)} %param.17) | copy-start | bytes 393220
Sparse Core Ops, SparseCore 0:
  12.8 62.6 all-gather.2
  94.4 201.4 reduce-scatter.1
  328.0 40.0 all-gather.4
where the time goes:
time: 431 us; the launch traced here: 430 us
  waiting for transfers between devices  292 us (68%)
  local copies, waits for them, and re-layouts  44.4 us (10%)
  blocking collectives  40.1 us (9%)
  matrix products  21.2 us (5%)
  between operations  13.4 us (3%)
  other arithmetic  10.3 us (2%)
  starting transfers between devices  8.47 us (2%)
    reduce_scatter x1, waiting for transfers between devices, shards(): lax.psum_scatter(jnp.transpose(summed_part, (1, 2, 0)), COL, scatter_dime...  200 us
    all_gather x1, waiting for transfers between devices, shards(): right_columns = lax.all_gather(right_factor, ROW, axis=0, tiled=True)  62.3 us
    convert_element_type x5, local copies, waits for them, and re-layouts, attend_dense(): scores = scores + head_bias.astype(jnp.float32)[None]  26.8 us
    all_gather x3, blocking collectives, gather_in_order(): pieces = lax.all_gather(pieces, axes[k], axis=0, tiled=True)  23.7 us
    all_gather x1, waiting for transfers between devices, gather_in_order(): pieces = lax.all_gather(pieces, axes[k], axis=0, tiled=True)  20.3 us
    all_to_all x1, blocking collectives, shards(): lax.all_to_all(attended_rows, COL, split_axis=2, concat_axis=0, tiled=True)  16.3 us
    transpose x1, local copies, waits for them, and re-layouts, shards(): jnp.transpose(summed_part, (1, 2, 0))  9.81 us
    all_to_all x1, waiting for transfers between devices, shards(): lax.all_to_all(grouped, COL, split_axis=0, concat_axis=2, tiled=True)  9.35 us
  transfers between devices with their start and end apart: 4, of which 4 were waited for; matrix products, arithmetic and copies ran while one was open for 1% of the time, Pallas kernels for 0%

commit v1 on v0

v1 whole, which is shorter than its diff:
```python
import functools
import math

import jax
import jax.numpy as jnp
import numpy as np
from jax import lax
from jax.experimental import pallas as pl
from jax.experimental.pallas import tpu as pltpu
from jax.sharding import PartitionSpec as P

MESH = pl.DeviceIdType.MESH
F32 = jnp.float32
BF16 = jnp.bfloat16
EPS = 1e-05
ROWS, COLS, C, N = 8, 16, 128, 384
HEADS, WIDTH = 4, 32
ZS, GS, OWN = 8, 16, 3
LOG2E = 1.4426950408889634
MASKED = -1e30


def dot(a, b):
    return jnp.dot(a, b, preferred_element_type=F32)


def dot_nt(a, b):
    return lax.dot_general(a, b, (((1,), (1,)), ((), ())), preferred_element_type=F32)


def dot_tn(a, b):
    return lax.dot_general(a, b, (((0,), (0,)), ((), ())), preferred_element_type=F32)


def wide(gain):
    return jnp.concatenate([gain] * (N // 128), axis=1)


def norm_columns(v, gain):
    centered = v - jnp.mean(v, axis=0, keepdims=True)
    variance = jnp.mean(centered * centered, axis=0, keepdims=True)
    return centered * lax.rsqrt(variance + EPS) * wide(gain)


def sigmoid(v):
    return 1.0 / (1.0 + jnp.exp(-v))


def turned(w):
    return jnp.transpose(w.astype(F32))


def kernel(
    x_ref, mask_ref, pattern_ref, perm_ref,
    norm1_ref, w_in_ref, w_gate_ref, norm2_ref, w_out1_ref,
    norm3_ref, w_qkv_ref, w_gate2_ref, w_bias_ref, w_out2_ref,
    out_ref,
    x_rows, send_l, recv_l, send_z, recv_z, send_p, recv_p, send_x, recv_x,
    bias_all, bias_full, send_o, xt, gate1, mid, an_t, wide_t, bias_t, penalty,
    w_g, w_v, w_gate_t, w_o1_t, w_qv_t, w_k_t, w_gate2_t, w_o2_t, gains,
    r_send, r_recv, l_send, l_recv, z_send, z_recv, p_send, p_recv, x_send, x_recv,
    bz_send, bz_recv, bx_send, bx_recv, by_send, by_recv, o_send, o_recv, local,
):
    row, col = lax.axis_index("row"), lax.axis_index("col")
    z, x_lo = col // 2, col % 2
    x_hi, y = row // 4, row % 4
    g = row * 2 + x_lo
    x_at = x_hi * 2 + x_lo

    def remote(src, dst, send, recv, r, c):
        return pltpu.make_async_remote_copy(
            src_ref=src, dst_ref=dst, send_sem=send, recv_sem=recv,
            device_id={"row": r, "col": c}, device_id_type=MESH,
        )

    def xy_place(other):
        return other // 2, z * 2 + other % 2

    barrier = pltpu.get_barrier_semaphore()
    for d in range(1, COLS):
        pl.semaphore_signal(barrier, inc=1, device_id={"row": row, "col": lax.rem(col + d, COLS)}, device_id_type=MESH)
    for d in range(1, ROWS):
        for e in range(2):
            pl.semaphore_signal(barrier, inc=1, device_id={"row": lax.rem(row + d, ROWS), "col": z * 2 + e}, device_id_type=MESH)

    w_t = jnp.concatenate([turned(w_in_ref[:, s * C : (s + 1) * C]) for s in range(4)], axis=0)
    ga, va, gb, vb = (w_t[s * C : (s + 1) * C].reshape(GS, 8, C) for s in range(4))
    w_g[...] = jnp.concatenate([ga, gb], axis=1).reshape(2 * C, C).astype(BF16)
    w_v[...] = jnp.concatenate([va, vb], axis=1).reshape(2 * C, C).astype(BF16)
    for slot, ref in enumerate((norm1_ref, norm2_ref, norm3_ref)):
        gains[slot] = jnp.transpose(jnp.broadcast_to(ref[...], (C, C)))

    pl.semaphore_wait(barrier, COLS - 1 + 2 * (ROWS - 1))

    def r_copy(d):
        peer = lax.rem(col + d, COLS)
        return remote(x_ref.at[pl.ds(OWN * peer, OWN)], x_rows.at[col], r_send.at[peer], r_recv.at[col], row, peer)

    def r_arrival(d):
        peer = lax.rem(col + d, COLS)
        return remote(x_ref.at[pl.ds(OWN * peer, OWN)], x_rows.at[peer], r_send.at[peer], r_recv.at[peer], row, peer)

    for d in range(1, COLS):
        r_copy(d).start()
    own_rows = pltpu.make_async_copy(x_ref.at[pl.ds(OWN * col, OWN)], x_rows.at[col], local.at[0])
    own_rows.start()

    w_gate_t[...] = turned(w_gate_ref[...]).astype(BF16)
    w_o1_t[...] = turned(w_out1_ref[...]).astype(BF16)
    w_o2_t[...] = turned(w_out2_ref[...]).astype(BF16)
    w_gate2_t[...] = turned(w_gate2_ref[...]).astype(BF16)
    w_qv_t[0] = turned(w_qkv_ref[:, :C]).astype(BF16)
    w_qv_t[1] = turned(w_qkv_ref[:, 2 * C :]).astype(BF16)
    w_k_t[...] = turned(w_qkv_ref[:, C : 2 * C]).astype(BF16)
    mask = mask_ref[...].astype(F32)
    lane = lax.broadcasted_iota(jnp.int32, (1, N), 1)
    key_mask = jnp.transpose(jnp.broadcast_to(mask, (C, N)))
    for b in range(4):
        line = jnp.zeros((1, N), F32)
        for a in range(4):
            inside = (lane >= 96 * a) & (lane < 96 * (a + 1))
            line = line + jnp.where(inside, pattern_ref[a, b].astype(F32), 0.0)
        part = wide(key_mask[96 * b : 96 * (b + 1)]) * line
        penalty[96 * b : 96 * (b + 1), :] = jnp.where(part > 0.0, 0.0, MASKED)

    own_rows.wait()
    for d in range(1, COLS):
        r_arrival(d).wait_recv()

    def l_copy(i, d, arriving):
        peer = lax.rem(g + d, GS)
        r, c = xy_place(peer)
        slot = peer if arriving else g
        return remote(send_l.at[i, peer], recv_l.at[i, slot], l_send.at[i, peer], l_recv.at[i, slot], r, c)

    def l_own(i):
        return pltpu.make_async_copy(send_l.at[i, g], recv_l.at[i, g], local.at[i])

    for i in range(OWN):
        x_t = jnp.transpose(x_rows[:, i].astype(F32).reshape(N, C))
        xt[i] = x_t
        normed = norm_columns(x_t, gains[0]).astype(BF16)
        an_t[i] = normed
        own_token = row * 48 + col * OWN + i
        mine = jnp.sum(jnp.where(lane == own_token, mask, 0.0), axis=1, keepdims=True)
        factors = sigmoid(dot(w_g[...], normed)) * dot(w_v[...], normed) * (mask * mine)
        send_l[i] = factors.astype(BF16).reshape(GS, 16, N)
        for d in range(1, GS):
            l_copy(i, d, False).start()
        l_own(i).start()
    for i in range(OWN):
        gate1[i] = sigmoid(dot(w_gate_t[...], an_t[i]))
    for d in range(1, COLS):
        r_copy(d).wait_send()

    for i in range(OWN):
        l_own(i).wait()
        for d in range(1, GS):
            l_copy(i, d, True).wait_recv()
        arrived = recv_l[i].astype(F32).reshape(GS * 16, N)
        for b in range(3):
            wide_t[b, i * 256 : (i + 1) * 256, :] = arrived[:, b * 128 : (b + 1) * 128]
    for ch in range(16):
        for b in range(3):
            piece = wide_t[b, pl.ds(ch, 48, stride=16), :]
            send_z[ch % 8, ch // 8, :, b * 128 : (b + 1) * 128] = piece.astype(BF16)

    def z_copy(src, dst, send, recv, d, arriving):
        peer = lax.rem(z + d, ZS)
        slot = peer if arriving else z
        return remote(src.at[peer], dst.at[slot], send.at[peer], recv.at[slot], row, peer * 2 + x_lo)

    for d in range(1, ZS):
        z_copy(send_z, recv_z, z_send, z_recv, d, False).start()
    own_z = pltpu.make_async_copy(send_z.at[z], recv_z.at[z], local.at[0])
    own_z.start()
    for i in range(OWN):
        for d in range(1, GS):
            l_copy(i, d, False).wait_send()
    own_z.wait()
    for d in range(1, ZS):
        z_copy(send_z, recv_z, z_send, z_recv, d, True).wait_recv()

    left = recv_z[:, 0].reshape(N, N)
    right = dot(perm_ref[...], recv_z[:, 1].reshape(N, N)).astype(BF16)
    send_p[...] = dot_nt(left, right).astype(BF16).reshape(ZS, 48, N)
    for d in range(1, ZS):
        z_copy(send_p, recv_p, p_send, p_recv, d, False).start()
    own_p = pltpu.make_async_copy(send_p.at[z], recv_p.at[z], local.at[0])
    own_p.start()
    for d in range(1, ZS):
        z_copy(send_z, recv_z, z_send, z_recv, d, False).wait_send()
    own_p.wait()
    for d in range(1, ZS):
        z_copy(send_p, recv_p, p_send, p_recv, d, True).wait_recv()

    arrived = recv_p[...].astype(F32).reshape(N, N)
    for b in range(3):
        wide_t[b, :N, :] = arrived[:, b * 128 : (b + 1) * 128]
    for i in range(OWN):
        for other in range(GS):
            for b in range(3):
                piece = wide_t[b, pl.ds(i * GS + other, 8, stride=48), :]
                send_x[other, i, :, b * 128 : (b + 1) * 128] = piece.astype(BF16)

    def x_copy(d, arriving):
        peer = lax.rem(g + d, GS)
        r, c = xy_place(peer)
        slot = peer if arriving else g
        return remote(send_x.at[peer], recv_x.at[slot], x_send.at[peer], x_recv.at[slot], r, c)

    for d in range(1, GS):
        x_copy(d, False).start()
    own_x = pltpu.make_async_copy(send_x.at[g], recv_x.at[g], local.at[0])
    own_x.start()
    for d in range(1, ZS):
        z_copy(send_p, recv_p, p_send, p_recv, d, False).wait_send()
    own_x.wait()
    for d in range(1, GS):
        x_copy(d, True).wait_recv()

    for i in range(OWN):
        product = recv_x[:, i].astype(F32).reshape(C, N)
        update = dot(w_o1_t[...], norm_columns(product, gains[1]).astype(BF16))
        middle = (xt[i] + gate1[i] * update).astype(BF16).astype(F32)
        mid[i] = middle
        attend = norm_columns(middle, gains[2]).astype(BF16)
        an_t[i] = attend
        bias_all[x_at, z, i] = dot_tn(w_bias_ref[...], attend).astype(BF16)

    def bz_copy(d, arriving):
        peer = lax.rem(z + d, ZS)
        slot = peer if arriving else z
        return remote(bias_all.at[x_at, z], bias_all.at[x_at, slot], bz_send.at[peer], bz_recv.at[slot], row, peer * 2 + x_lo)

    for d in range(1, ZS):
        bz_copy(d, False).start()

    def x_place(at):
        return (at // 2) * 4 + y, z * 2 + at % 2

    up, down = lax.rem(x_at + 1, 4), lax.rem(x_at + 3, 4)
    opposite = lax.rem(x_at + 2, 4)

    def bx_copy(k, arriving):
        target = up if k % 2 == 0 else down
        if k < 2:
            held = (down if k == 0 else up) if arriving else x_at
            ref = bias_all.at[held]
        else:
            held = opposite if arriving else (down if k == 2 else up)
            ref = bias_all.at[held, 4 * (k - 2) : 4 * (k - 1)]
        r, c = x_place(target)
        return remote(ref, ref, bx_send.at[k], bx_recv.at[k], r, c)

    for d in range(1, ZS):
        bz_copy(d, True).wait_recv()
    for k in range(2):
        bx_copy(k, False).start()
    for k in range(2):
        bx_copy(k, True).wait_recv()
        bx_copy(k + 2, False).start()
    for k in range(2, 4):
        bx_copy(k, True).wait_recv()

    for hi in range(2):
        for zz in range(ZS):
            for lo in range(2):
                for i in range(OWN):
                    piece = bias_all[2 * hi + lo, zz, i].astype(F32)
                    at = (((hi * ZS + zz) * 2 + lo) * OWN + i) * 4
                    for b in range(3):
                        wide_t[b, at : at + 4, :] = piece[:, b * 128 : (b + 1) * 128]
    for hi in range(2):
        for h in range(HEADS):
            for b in range(3):
                piece = wide_t[b, pl.ds(hi * 192 + h, 48, stride=4), :]
                bias_full[h, hi, y, :, b * 128 : (b + 1) * 128] = piece.astype(BF16)

    y_up, y_down, y_far = lax.rem(y + 1, 4), lax.rem(y + 3, 4), lax.rem(y + 2, 4)

    def by_copy(k, arriving):
        target = y_up if k % 2 == 0 else y_down
        if k < 2:
            held = (y_down if k == 0 else y_up) if arriving else y
            ref = bias_full.at[:, :, held]
        else:
            held = y_far if arriving else (y_down if k == 2 else y_up)
            ref = bias_full.at[:, k - 2, held]
        return remote(ref, ref, by_send.at[k], by_recv.at[k], x_hi * 4 + target, col)

    for k in range(2):
        by_copy(k, False).start()

    for d in range(1, GS):
        x_copy(d, False).wait_send()

    for k in range(2):
        by_copy(k, True).wait_recv()
        by_copy(k + 2, False).start()
    for k in range(2, 4):
        by_copy(k, True).wait_recv()
    for h in range(HEADS):
        whole = bias_full[h].reshape(N, N).astype(F32)
        bias_t[h] = jnp.transpose(whole) * LOG2E + penalty[...]

    def o_copy(i, d, arriving):
        peer = lax.rem(col + d, COLS)
        slot = peer if arriving else col
        return remote(send_o.at[i, peer], out_ref.at[OWN * slot + i], o_send.at[i, peer], o_recv.at[i, slot], row, peer)

    def o_own(i):
        return pltpu.make_async_copy(send_o.at[i, col], out_ref.at[OWN * col + i], local.at[i])

    scale = LOG2E / math.sqrt(WIDTH)
    head_of = lax.broadcasted_iota(jnp.int32, (C, N), 0)
    for i in range(OWN):
        attend = an_t[i]
        queries = dot(w_qv_t[0], attend) * scale
        values = dot(w_qv_t[1], attend).astype(BF16)
        keys = jnp.transpose(dot(w_k_t[...], attend)).astype(BF16)
        gate2 = sigmoid(dot(w_gate2_t[...], attend))
        parts = []
        for h in range(HEADS):
            inside = (head_of >= WIDTH * h) & (head_of < WIDTH * (h + 1))
            own_queries = jnp.where(inside, queries, 0.0).astype(BF16)
            scores = dot(keys, own_queries) + bias_t[h]
            weights = jnp.exp2(scores - jnp.max(scores, axis=0, keepdims=True))
            total = jnp.sum(weights, axis=0, keepdims=True)
            mixed = dot(values[WIDTH * h : WIDTH * (h + 1)], weights.astype(BF16))
            parts.append(mixed / total)
        gated = (gate2 * jnp.concatenate(parts, axis=0)).astype(BF16)
        result = mid[i] + dot(w_o2_t[...], gated)
        send_o[i] = jnp.transpose(result).reshape(COLS, 24, C).astype(BF16)
        for d in range(1, COLS):
            o_copy(i, d, False).start()
        o_own(i).start()

    for d in range(1, ZS):
        bz_copy(d, False).wait_send()
    for k in range(4):
        bx_copy(k, False).wait_send()
        by_copy(k, False).wait_send()
    for i in range(OWN):
        o_own(i).wait()
        for d in range(1, COLS):
            o_copy(i, d, True).wait_recv()
    for i in range(OWN):
        for d in range(1, COLS):
            o_copy(i, d, False).wait_send()


def token_order():
    perm = np.zeros((N, N), np.float32)
    for t in range(N):
        r, c, i = t // 48, (t % 48) // 3, t % 3
        perm[t, (c // 2) * 48 + i * GS + 2 * r + c % 2] = 1.0
    return perm


def shards(
    pair_state, token_mask, block_pattern, triangle_norm, triangle_input, triangle_gate, product_norm,
    triangle_output, attend_norm, attend_inputs, attend_gate, attend_bias, attend_output,
):
    vmem = pl.BlockSpec(memory_space=pltpu.VMEM)
    smem = pl.BlockSpec(memory_space=pltpu.SMEM)
    dma = pltpu.SemaphoreType.DMA
    V = pltpu.VMEM
    return pl.pallas_call(
        kernel,
        out_shape=jax.ShapeDtypeStruct(pair_state.shape, BF16),
        in_specs=[vmem, vmem, smem] + [vmem] * 11,
        out_specs=vmem,
        scratch_shapes=[
            V((COLS, OWN, 24, C), BF16),
            V((OWN, GS, 16, N), BF16), V((OWN, GS, 16, N), BF16),
            V((ZS, 2, 48, N), BF16), V((ZS, 2, 48, N), BF16),
            V((ZS, 48, N), BF16), V((ZS, 48, N), BF16),
            V((GS, OWN, 8, N), BF16), V((GS, OWN, 8, N), BF16),
            V((4, ZS, OWN, HEADS, N), BF16),
            V((HEADS, 2, 4, 48, N), BF16),
            V((OWN, COLS, 24, C), BF16),
            V((OWN, C, N), F32), V((OWN, C, N), F32), V((OWN, C, N), F32), V((OWN, C, N), BF16),
            V((3, 768, 128), F32), V((HEADS, N, N), F32), V((N, N), F32),
            V((2 * C, C), BF16), V((2 * C, C), BF16), V((C, C), BF16), V((C, C), BF16),
            V((2, C, C), BF16), V((C, C), BF16), V((C, C), BF16), V((C, C), BF16), V((3, C, C), F32),
            dma((COLS,)), dma((COLS,)), dma((OWN, GS)), dma((OWN, GS)), dma((ZS,)), dma((ZS,)),
            dma((ZS,)), dma((ZS,)), dma((GS,)), dma((GS,)),
            dma((ZS,)), dma((ZS,)), dma((4,)), dma((4,)), dma((4,)), dma((4,)),
            dma((OWN, COLS)), dma((OWN, COLS)), dma((4,)),
        ],
        compiler_params=pltpu.CompilerParams(
            collective_id=0, has_side_effects=True, vmem_limit_bytes=60 * 1024 * 1024
        ),
        name="pairformer",
    )(
        pair_state, token_mask.reshape(1, N), block_pattern, jnp.asarray(token_order(), BF16),
        triangle_norm.reshape(1, C), triangle_input, triangle_gate, product_norm.reshape(1, C), triangle_output,
        attend_norm.reshape(1, C), attend_inputs, attend_gate, attend_bias, attend_output,
    )


def solution(mesh):
    tile = P(("crop", "row"), "col", None)
    return jax.shard_map(
        shards,
        mesh=mesh,
        in_specs=(tile, P("crop"), P("crop", None)) + (P(),) * 10,
        out_specs=tile,
        check_vma=False,
    )
```

time: 431 us -> 102 us (0.24)
  waiting for transfers between devices: 292 us -> 0 us
  Pallas kernels: 0 us -> 97.6 us
  local copies, waits for them, and re-layouts: 44.4 us -> 3.8 us
  blocking collectives: 40.1 us -> 0 us
  matrix products: 21.2 us -> 0 us
  between operations: 13.4 us -> 0.01 us
  other arithmetic: 10.3 us -> 0 us
  starting transfers between devices: 8.47 us -> 0 us
    reduce_scatter x1 -> x0, waiting for transfers between devices: 200 us -> none  [shards(): lax.psum_scatter(jnp.transpose(summed_part, (1, 2, 0)), COL, scatter_dime...]
    pallas_call x0 -> x1, Pallas kernels: none -> 97.6 us  [shards(): pl.pallas_call(kernel, out_shape=jax.ShapeDtypeStruct(pair_state.shape, B...]
    all_gather x2 -> x0, waiting for transfers between devices: 82.6 us -> none  [the longest x1 62.3 us: shards(): right_columns = lax.all_gather(right_factor, ROW, axis=0, tiled=True)]
    convert_element_type x7 -> x0, local copies, waits for them, and re-layouts: 27.3 us -> none  [the longest x5 26.8 us: attend_dense(): scores = scores + head_bias.astype(jnp.float32)[None]]
    all_gather x3 -> x0, blocking collectives: 23.7 us -> none  [gather_in_order(): pieces = lax.all_gather(pieces, axes[k], axis=0, tiled=True)]
    all_to_all x1 -> x0, blocking collectives: 16.3 us -> none  [shards(): lax.all_to_all(attended_rows, COL, split_axis=2, concat_axis=0, tiled=True)]
    dot_general x9 -> x0, matrix products: 14.6 us -> none  [the longest x1 5.07 us: shards(): lax.dot_general(right_columns, left_factor, (((1,), (1,)), ((2,), (2,))),...]
    transpose x1 -> x0, local copies, waits for them, and re-layouts: 9.81 us -> none  [shards(): jnp.transpose(summed_part, (1, 2, 0))]
  transfers between devices with their start and end apart: 4 -> 0, of which waited for: 4 -> 0; matrix products, arithmetic and copies ran while one was open for 1% -> 0% of each run, Pallas kernels for 0% -> 0%
where the time goes in v1:
time: 102 us; the launch traced here: 101 us
  Pallas kernels  97.6 us (96%)
  local copies, waits for them, and re-layouts  3.8 us (4%)
    pallas_call x1, Pallas kernels, shards(): pl.pallas_call(kernel, out_shape=jax.ShapeDtypeStruct(pair_state.shape, B...  97.6 us
    unnamed x6, local copies, waits for them, and re-layouts  3.21 us

profile of v1, /device:TPU:2, one launch (start us, length us, event | category | flops | bytes accessed | tf_op | source)
XLA Modules:
  0.0 101.4 jit_solution(5694644836250696960)
XLA Ops:
  0.0 0.0 copy-start
  0.0 0.7 copy-done
  0.7 0.0 copy-start.1
  0.7 0.6 reshape.12.mask_ref
  1.3 0.1 copy-done.1
  1.4 0.7 copy.15.w_bias_ref
  2.1 97.6 %pairformer.1 = bf16[48,24,128]{2,1,0:T(8,128)(2,1)} custom-call(bf16[48,24,128]{2,1,0:T(8,128)(2,1)} %x_ref.1, s32[1,384]{1,0:T(1,128)} %reshape.12.mask_ref, s32[4,4]{1,0:T(4,128)} %pattern_ref.1, bf16[384,384]{1,0:T(8,128)(2,1)} %constant.2.clone.perm_ref, f32[1,128]{1,0:T(1,128)} %bitcast.3, bf16[128,512]{1,0:T(8,128)(2,1)} %w_in_ref.1, ...), custom_call_target="tpu_custom_call" | custom-call | tf_op jit(solution)/shard_map/pairformer/pallas_call | solution.py:369
  99.7 1.7 %copy.17 = bf16[48,24,128]{2,1,0:T(8,128)(2,1)} copy(bf16[48,24,128]{2,1,0:T(8,128)(2,1)} %pairformer.1) | data formatting | bytes 589824
Async XLA Ops:
  0.0 0.7 copy-start
  0.7 0.7 copy-start.1

commit v2 on v1

v2 whole, which is shorter than its diff:
```python
import functools
import math

import jax
import jax.numpy as jnp
import numpy as np
from jax import lax
from jax.experimental import pallas as pl
from jax.experimental.pallas import tpu as pltpu
from jax.sharding import PartitionSpec as P

MESH = pl.DeviceIdType.MESH
F32 = jnp.float32
BF16 = jnp.bfloat16
EPS = 1e-05
ROWS, COLS, C, N = 8, 16, 128, 384
HEADS, WIDTH = 4, 32
ZS, GS, OWN = 8, 16, 3
LOG2E = 1.4426950408889634
MASKED = -1e30


def dot(a, b):
    return jnp.dot(a, b, preferred_element_type=F32)


def dot_nt(a, b):
    return lax.dot_general(a, b, (((1,), (1,)), ((), ())), preferred_element_type=F32)


def dot_tn(a, b):
    return lax.dot_general(a, b, (((0,), (0,)), ((), ())), preferred_element_type=F32)


def wide(gain):
    return jnp.concatenate([gain] * (N // 128), axis=1)


def norm_columns(v, gain):
    centered = v - jnp.mean(v, axis=0, keepdims=True)
    variance = jnp.mean(centered * centered, axis=0, keepdims=True)
    return centered * lax.rsqrt(variance + EPS) * wide(gain)


def sigmoid(v):
    return 1.0 / (1.0 + jnp.exp(-v))


def turned(w):
    return jnp.transpose(w.astype(F32))


RING_STEPS = (2, 1, 3)
Z_STEPS = (4, 3, 5, 2, 6, 1, 7)
COL_STEPS = tuple((dz, dl) for dz in Z_STEPS for dl in (1, 0)) + ((0, 1),)
XY_STEPS = tuple(sorted(
    ((dx, dy) for dx in range(4) for dy in range(4) if dx or dy),
    key=lambda s: -(min(s[0], 4 - s[0]) + min(s[1], 4 - s[1])),
))


def kernel(
    x_hbm, mask_ref, pattern_ref, perm_hbm,
    norm1_ref, w_in_hbm, w_gate_hbm, norm2_ref, w_out1_hbm,
    norm3_ref, w_qkv_hbm, w_gate2_hbm, w_bias_ref, w_out2_hbm,
    out_ref,
    x_rows, send_l, recv_l, send_z, recv_z, send_p, recv_p, send_x, recv_x,
    bias_all, send_o, xt, gate1, mid, an_t, wide_t, bias_t, penalty, scores_ref, values_ref, gate2_ref,
    perm_ref, w_in_ref, w_gate_ref, w_out1_ref, w_qkv_ref, w_gate2_ref, w_out2_ref,
    w_g, w_v, w_gate_t, w_o1_t, w_qv_t, w_k_t, w_gate2_t, w_o2_t, gains,
    r_send, r_recv, l_send, l_recv, z_send, z_recv, p_send, p_recv, x_send, x_recv,
    bz_send, bz_recv, ba_send, ba_recv, bb_send, bb_recv, o_send, o_recv, local, fetch,
):
    crop, row, col = lax.axis_index("crop"), lax.axis_index("row"), lax.axis_index("col")
    z, x_lo = col // 2, col % 2
    x_hi, y = row // 4, row % 4
    g = row * 2 + x_lo
    x_at = x_hi * 2 + x_lo

    def place(x, y, z):
        return (x // 2) * 4 + y, z * 2 + x % 2

    def signal(r, c):
        pl.semaphore_signal(barrier, inc=1, device_id={"row": r, "col": c}, device_id_type=MESH)

    def remote(src, dst, send, recv, r, c):
        return pltpu.make_async_remote_copy(
            src_ref=src, dst_ref=dst, send_sem=send, recv_sem=recv,
            device_id={"row": r, "col": c}, device_id_type=MESH,
        )

    def col_peer(dz, dl):
        return lax.rem(z + dz, ZS) * 2 + lax.rem(x_lo + dl, 2)

    def xy_peer(dx, dy):
        xx, yy = lax.rem(x_at + dx, 4), lax.rem(y + dy, 4)
        r, c = place(xx, yy, z)
        return r * 2 + xx % 2, r, c

    barrier = pltpu.get_barrier_semaphore()
    for dz, dl in COL_STEPS:
        signal(row, col_peer(dz, dl))
    for dx, dy in XY_STEPS:
        if (dx, dy) != (1, 0) and (dx, dy) != (3, 0) and (dx, dy) != (2, 0):
            _, r, c = xy_peer(dx, dy)
            signal(r, c)
    _, r, c = xy_peer(2, 0)
    signal(r, c)
    far = x_at + 1 + 2 * (1 - x_at % 2)
    r, c = place(lax.rem(far, 4), y, z)
    signal(r, c)

    fetched = [
        pltpu.make_async_copy(src, dst, fetch.at[n])
        for n, (src, dst) in enumerate((
            (w_in_hbm, w_in_ref), (w_gate_hbm, w_gate_ref), (w_out1_hbm, w_out1_ref), (w_qkv_hbm, w_qkv_ref),
            (w_gate2_hbm, w_gate2_ref), (w_out2_hbm, w_out2_ref), (perm_hbm, perm_ref),
        ))
    ]
    for copy in fetched:
        copy.start()

    fetched[0].wait()
    w_t = jnp.concatenate([turned(w_in_ref[:, s * C : (s + 1) * C]) for s in range(4)], axis=0)
    ga, va, gb, vb = (w_t[s * C : (s + 1) * C].reshape(GS, 8, C) for s in range(4))
    w_g[...] = jnp.concatenate([ga, gb], axis=1).reshape(2 * C, C).astype(BF16)
    w_v[...] = jnp.concatenate([va, vb], axis=1).reshape(2 * C, C).astype(BF16)
    for slot, ref in enumerate((norm1_ref, norm2_ref, norm3_ref)):
        gains[slot] = jnp.transpose(jnp.broadcast_to(ref[...], (C, C)))

    pl.semaphore_wait(barrier, COLS - 1 + 2 * (ROWS - 1))

    def r_copy(i, dz, dl, arriving):
        peer = col_peer(dz, dl)
        slot = peer if arriving else col
        return remote(x_hbm.at[OWN * peer + i], x_rows.at[i, slot], r_send.at[i, peer], r_recv.at[i, slot], row, peer)

    def r_own(i):
        return pltpu.make_async_copy(x_hbm.at[OWN * col + i], x_rows.at[i, col], local.at[i])

    for i in range(OWN):
        for dz, dl in COL_STEPS:
            r_copy(i, dz, dl, False).start()
        r_own(i).start()

    for copy in fetched[1:6]:
        copy.wait()
    w_gate_t[...] = turned(w_gate_ref[...]).astype(BF16)
    w_o1_t[...] = turned(w_out1_ref[...]).astype(BF16)
    w_o2_t[...] = turned(w_out2_ref[...]).astype(BF16)
    w_gate2_t[...] = turned(w_gate2_ref[...]).astype(BF16)
    w_qv_t[0] = turned(w_qkv_ref[:, :C]).astype(BF16)
    w_qv_t[1] = turned(w_qkv_ref[:, 2 * C :]).astype(BF16)
    w_k_t[...] = turned(w_qkv_ref[:, C : 2 * C]).astype(BF16)
    mask = mask_ref[...].astype(F32)
    lane = lax.broadcasted_iota(jnp.int32, (1, N), 1)
    key_mask = jnp.transpose(jnp.broadcast_to(mask, (C, N)))
    for b in range(4):
        line = jnp.zeros((1, N), F32)
        for a in range(4):
            inside = (lane >= 96 * a) & (lane < 96 * (a + 1))
            line = line + jnp.where(inside, pattern_ref[a, b].astype(F32), 0.0)
        part = wide(key_mask[96 * b : 96 * (b + 1)]) * line
        penalty[96 * b : 96 * (b + 1), :] = jnp.where(part > 0.0, 0.0, MASKED)
    fetched[6].wait()

    def l_copy(i, dx, dy, arriving):
        peer, r, c = xy_peer(dx, dy)
        slot = peer if arriving else g
        return remote(send_l.at[i, peer], recv_l.at[i, slot], l_send.at[i, peer], l_recv.at[i, slot], r, c)

    def l_own(i):
        return pltpu.make_async_copy(send_l.at[i, g], recv_l.at[i, g], local.at[i])

    for i in range(OWN):
        r_own(i).wait()
        for dz, dl in COL_STEPS:
            r_copy(i, dz, dl, True).wait_recv()
        x_t = jnp.transpose(x_rows[i].astype(F32).reshape(N, C))
        xt[i] = x_t
        normed = norm_columns(x_t, gains[0]).astype(BF16)
        an_t[i] = normed
        own_token = row * 48 + col * OWN + i
        mine = jnp.sum(jnp.where(lane == own_token, mask, 0.0), axis=1, keepdims=True)
        factors = sigmoid(dot(w_g[...], normed)) * dot(w_v[...], normed) * (mask * mine)
        send_l[i] = factors.astype(BF16).reshape(GS, 16, N)
        for dx, dy in XY_STEPS:
            l_copy(i, dx, dy, False).start()
        l_own(i).start()
    for i in range(OWN):
        gate1[i] = sigmoid(dot(w_gate_t[...], an_t[i]))
    for i in range(OWN):
        for dz, dl in COL_STEPS:
            r_copy(i, dz, dl, False).wait_send()

    def z_copy(i, src, dst, send, recv, dz, arriving):
        peer = lax.rem(z + dz, ZS)
        slot = peer if arriving else z
        return remote(src.at[i, peer], dst.at[i, slot], send.at[i, peer], recv.at[i, slot], row, peer * 2 + x_lo)

    def z_own(i, src, dst):
        return pltpu.make_async_copy(src.at[i, z], dst.at[i, z], local.at[i])

    for i in range(OWN):
        l_own(i).wait()
        for dx, dy in XY_STEPS:
            l_copy(i, dx, dy, True).wait_recv()
        arrived = recv_l[i].astype(F32).reshape(GS * 16, N)
        for b in range(3):
            wide_t[b, i * 256 : (i + 1) * 256, :] = arrived[:, b * 128 : (b + 1) * 128]
        for ch in range(16):
            for b in range(3):
                piece = wide_t[b, pl.ds(i * 256 + ch, GS, stride=16), :]
                send_z[i, ch % 8, ch // 8, :, b * 128 : (b + 1) * 128] = piece.astype(BF16)
        for dz in Z_STEPS:
            z_copy(i, send_z, recv_z, z_send, z_recv, dz, False).start()
        z_own(i, send_z, recv_z).start()
    for i in range(OWN):
        for dx, dy in XY_STEPS:
            l_copy(i, dx, dy, False).wait_send()
    for i in range(OWN):
        z_own(i, send_z, recv_z).wait()
        for dz in Z_STEPS:
            z_copy(i, send_z, recv_z, z_send, z_recv, dz, True).wait_recv()

    right = dot(perm_ref[...], recv_z[:, :, 1].reshape(N, N)).astype(BF16)
    for i in range(OWN):
        left = recv_z[i, :, 0].reshape(ZS * GS, N)
        send_p[i] = dot_nt(left, right).astype(BF16).reshape(ZS, GS, N)
        for dz in Z_STEPS:
            z_copy(i, send_p, recv_p, p_send, p_recv, dz, False).start()
        z_own(i, send_p, recv_p).start()

    def x_copy(i, dx, dy, arriving):
        peer, r, c = xy_peer(dx, dy)
        slot = peer if arriving else g
        return remote(send_x.at[i, peer], recv_x.at[i, slot], x_send.at[i, peer], x_recv.at[i, slot], r, c)

    def x_own(i):
        return pltpu.make_async_copy(send_x.at[i, g], recv_x.at[i, g], local.at[i])

    for i in range(OWN):
        for dz in Z_STEPS:
            z_copy(i, send_z, recv_z, z_send, z_recv, dz, False).wait_send()
    for i in range(OWN):
        z_own(i, send_p, recv_p).wait()
        for dz in Z_STEPS:
            z_copy(i, send_p, recv_p, p_send, p_recv, dz, True).wait_recv()
        arrived = recv_p[i].astype(F32).reshape(ZS * GS, N)
        for b in range(3):
            wide_t[b, i * 128 : (i + 1) * 128, :] = arrived[:, b * 128 : (b + 1) * 128]
        for other in range(GS):
            for b in range(3):
                piece = wide_t[b, pl.ds(i * 128 + other, 8, stride=16), :]
                send_x[i, other, :, b * 128 : (b + 1) * 128] = piece.astype(BF16)
        for dx, dy in XY_STEPS:
            x_copy(i, dx, dy, False).start()
        x_own(i).start()

    b_at = y + crop * (x_at - y)
    a_at = x_at + crop * (y - x_at)
    for i in range(OWN):
        x_own(i).wait()
        for dx, dy in XY_STEPS:
            x_copy(i, dx, dy, True).wait_recv()
        product = recv_x[i].astype(F32).reshape(C, N)
        update = dot(w_o1_t[...], norm_columns(product, gains[1]).astype(BF16))
        middle = (xt[i] + gate1[i] * update).astype(BF16).astype(F32)
        mid[i] = middle
        attend = norm_columns(middle, gains[2]).astype(BF16)
        an_t[i] = attend
        bias_all[b_at, a_at, z, i] = dot(w_bias_ref[...], attend).astype(BF16)

    def bz_copy(dz, arriving):
        peer = lax.rem(z + dz, ZS)
        slot = peer if arriving else z
        return remote(
            bias_all.at[b_at, a_at, z], bias_all.at[b_at, a_at, slot], bz_send.at[peer], bz_recv.at[slot],
            row, peer * 2 + x_lo,
        )

    def ring_place(a, b):
        return place(a + crop * (b - a), b + crop * (a - b), z)

    def ba_copy(d, arriving):
        peer = lax.rem(a_at + d, 4)
        slot = peer if arriving else a_at
        r, c = ring_place(peer, b_at)
        return remote(bias_all.at[b_at, a_at], bias_all.at[b_at, slot], ba_send.at[peer], ba_recv.at[slot], r, c)

    def bb_copy(d, arriving):
        peer = lax.rem(b_at + d, 4)
        slot = peer if arriving else b_at
        r, c = ring_place(a_at, peer)
        return remote(bias_all.at[b_at], bias_all.at[slot], bb_send.at[peer], bb_recv.at[slot], r, c)

    for dz in Z_STEPS:
        bz_copy(dz, False).start()

    scale = LOG2E / math.sqrt(WIDTH)
    head_of = lax.broadcasted_iota(jnp.int32, (C, N), 0)

    def project(i):
        attend = an_t[i]
        queries = dot(w_qv_t[0], attend) * scale
        values_ref[i] = dot(w_qv_t[1], attend).astype(BF16)
        keys = jnp.transpose(dot(w_k_t[...], attend)).astype(BF16)
        gate2_ref[i] = sigmoid(dot(w_gate2_t[...], attend))
        for h in range(HEADS):
            inside = (head_of >= WIDTH * h) & (head_of < WIDTH * (h + 1))
            scores_ref[i, h] = dot(keys, jnp.where(inside, queries, 0.0).astype(BF16))

    project(0)
    for dz in Z_STEPS:
        bz_copy(dz, True).wait_recv()
    for d in RING_STEPS:
        ba_copy(d, False).start()
    project(1)
    for d in RING_STEPS:
        ba_copy(d, True).wait_recv()
    for d in RING_STEPS:
        bb_copy(d, False).start()
    project(2)
    for i in range(OWN):
        for dx, dy in XY_STEPS:
            x_copy(i, dx, dy, False).wait_send()
        for dz in Z_STEPS:
            z_copy(i, send_p, recv_p, p_send, p_recv, dz, False).wait_send()
    for d in RING_STEPS:
        bb_copy(d, True).wait_recv()
    for r in range(ROWS):
        for c in range(COLS):
            xx, yy = (r // 4) * 2 + c % 2, r % 4
            b_of, a_of = yy + crop * (xx - yy), xx + crop * (yy - xx)
            for i in range(OWN):
                piece = bias_all[b_of, a_of, c // 2, i].astype(F32)
                at = ((r * COLS + c) * OWN + i) * HEADS
                for b in range(3):
                    wide_t[b, at : at + HEADS, :] = piece[:, b * 128 : (b + 1) * 128]
    for h in range(HEADS):
        for b in range(3):
            part = wide_t[b, pl.ds(h, N, stride=HEADS), :]
            rows = slice(b * 128, (b + 1) * 128)
            bias_t[h, rows, :] = jnp.transpose(part) * LOG2E + penalty[rows, :]

    def o_copy(i, dz, dl, arriving):
        peer = col_peer(dz, dl)
        slot = peer if arriving else col
        return remote(send_o.at[i, peer], out_ref.at[OWN * slot + i], o_send.at[i, peer], o_recv.at[i, slot], row, peer)

    def o_own(i):
        return pltpu.make_async_copy(send_o.at[i, col], out_ref.at[OWN * col + i], local.at[i])

    for i in range(OWN):
        parts = []
        for h in range(HEADS):
            scores = scores_ref[i, h] + bias_t[h]
            weights = jnp.exp2(scores - jnp.max(scores, axis=0, keepdims=True))
            total = jnp.sum(weights, axis=0, keepdims=True)
            mixed = dot(values_ref[i, WIDTH * h : WIDTH * (h + 1)], weights.astype(BF16))
            parts.append(mixed / total)
        gated = (gate2_ref[i] * jnp.concatenate(parts, axis=0)).astype(BF16)
        result = mid[i] + dot(w_o2_t[...], gated)
        send_o[i] = jnp.transpose(result).reshape(COLS, 24, C).astype(BF16)
        for dz, dl in COL_STEPS:
            o_copy(i, dz, dl, False).start()
        o_own(i).start()

    for dz in Z_STEPS:
        bz_copy(dz, False).wait_send()
    for d in RING_STEPS:
        ba_copy(d, False).wait_send()
        bb_copy(d, False).wait_send()
    for i in range(OWN):
        o_own(i).wait()
        for dz, dl in COL_STEPS:
            o_copy(i, dz, dl, True).wait_recv()
    for i in range(OWN):
        for dz, dl in COL_STEPS:
            o_copy(i, dz, dl, False).wait_send()


def token_order():
    perm = np.zeros((N, N), np.float32)
    for t in range(N):
        r, c, i = t // 48, (t % 48) // 3, t % 3
        perm[t, i * ZS * GS + (c // 2) * GS + 2 * r + c % 2] = 1.0
    return perm


def shards(
    pair_state, token_mask, block_pattern, triangle_norm, triangle_input, triangle_gate, product_norm,
    triangle_output, attend_norm, attend_inputs, attend_gate, attend_bias, attend_output,
):
    vmem = pl.BlockSpec(memory_space=pltpu.VMEM)
    hbm = pl.BlockSpec(memory_space=pl.ANY)
    smem = pl.BlockSpec(memory_space=pltpu.SMEM)
    dma = pltpu.SemaphoreType.DMA
    V = pltpu.VMEM
    return pl.pallas_call(
        kernel,
        out_shape=jax.ShapeDtypeStruct(pair_state.shape, BF16),
        in_specs=[hbm, vmem, smem, hbm, vmem, hbm, hbm, vmem, hbm, vmem, hbm, hbm, vmem, hbm],
        out_specs=hbm,
        scratch_shapes=[
            V((OWN, COLS, 24, C), BF16),
            V((OWN, GS, 16, N), BF16), V((OWN, GS, 16, N), BF16),
            V((OWN, ZS, 2, GS, N), BF16), V((OWN, ZS, 2, GS, N), BF16),
            V((OWN, ZS, GS, N), BF16), V((OWN, ZS, GS, N), BF16),
            V((OWN, GS, 8, N), BF16), V((OWN, GS, 8, N), BF16),
            V((4, 4, ZS, OWN, HEADS, N), BF16),
            V((OWN, COLS, 24, C), BF16),
            V((OWN, C, N), F32), V((OWN, C, N), F32), V((OWN, C, N), F32), V((OWN, C, N), BF16),
            V((3, HEADS * N, 128), F32), V((HEADS, N, N), F32), V((N, N), F32),
            V((OWN, HEADS, N, N), F32), V((OWN, C, N), BF16), V((OWN, C, N), F32),
            V((N, N), BF16), V((C, 4 * C), BF16), V((C, C), BF16), V((C, C), BF16),
            V((C, 3 * C), BF16), V((C, C), BF16), V((C, C), BF16),
            V((2 * C, C), BF16), V((2 * C, C), BF16), V((C, C), BF16), V((C, C), BF16),
            V((2, C, C), BF16), V((C, C), BF16), V((C, C), BF16), V((C, C), BF16), V((3, C, C), F32),
            dma((OWN, COLS)), dma((OWN, COLS)), dma((OWN, GS)), dma((OWN, GS)), dma((OWN, ZS)), dma((OWN, ZS)),
            dma((OWN, ZS)), dma((OWN, ZS)), dma((OWN, GS)), dma((OWN, GS)),
            dma((ZS,)), dma((ZS,)), dma((4,)), dma((4,)), dma((4,)), dma((4,)),
            dma((OWN, COLS)), dma((OWN, COLS)), dma((OWN,)), dma((7,)),
        ],
        compiler_params=pltpu.CompilerParams(
            collective_id=0, has_side_effects=True, vmem_limit_bytes=40 * 1024 * 1024
        ),
        name="pairformer",
    )(
        pair_state, token_mask.reshape(1, N), block_pattern, jnp.asarray(token_order(), BF16),
        triangle_norm.reshape(1, C), triangle_input, triangle_gate, product_norm.reshape(1, C), triangle_output,
        attend_norm.reshape(1, C), attend_inputs, attend_gate, attend_bias.T, attend_output,
    )


def solution(mesh):
    tile = P(("crop", "row"), "col", None)
    return jax.shard_map(
        shards,
        mesh=mesh,
        in_specs=(tile, P("crop"), P("crop", None)) + (P(),) * 10,
        out_specs=tile,
        check_vma=False,
    )
```

time: 102 us -> 91.2 us (0.89)
  Pallas kernels: 97.6 us -> 81.8 us
  local copies, waits for them, and re-layouts: 3.8 us -> 8.82 us
    pallas_call x1, Pallas kernels: 97.6 us -> 81.8 us  [shards(): pl.pallas_call(kernel, out_shape=jax.ShapeDtypeStruct(pair_state.shape, B...]
    unnamed x6 -> x29, local copies, waits for them, and re-layouts: 3.21 us -> 8.82 us
where the time goes in v2:
time: 91.2 us; the launch traced here: 90.7 us
  Pallas kernels  81.8 us (90%)
  local copies, waits for them, and re-layouts  8.82 us (10%)
    pallas_call x1, Pallas kernels, shards(): pl.pallas_call(kernel, out_shape=jax.ShapeDtypeStruct(pair_state.shape, B...  81.8 us
    unnamed x29, local copies, waits for them, and re-layouts  8.82 us

profile of v2, /device:TPU:2, one launch (start us, length us, event | category | flops | bytes accessed | tf_op | source)
XLA Modules:
  0.0 90.7 jit_solution(13706670006128887240)
XLA Ops:
  0.0 0.0 copy-start.13
  0.0 0.0 copy-start.11
  0.0 0.0 copy-start.12
  0.0 0.7 copy-done.13
  0.7 0.0 copy-start.8
  0.7 0.0 copy-start.9
  0.7 0.0 copy-done.11
  0.7 0.0 copy-done.12
  0.7 0.7 copy-done.8
  1.4 0.0 copy-done.9
  1.4 0.0 copy-done.10
  1.4 0.0 copy-start
  1.4 1.0 %copy-done = bf16[48,24,128]{2,1,0:T(8,128)(2,1)S(1)} copy-done((bf16[48,24,128]{2,1,0:T(8,128)(2,1)S(1)}, bf16[48,24,128]{2,1,0:T(8,128)(2,1)}, u32[]{:S(2)}) %copy-start) | copy-done | bytes 294936
  2.3 0.0 copy-start.1
  2.3 1.0 %copy-done.1 = bf16[384,384]{1,0:T(8,128)(2,1)S(1)} copy-done((bf16[384,384]{1,0:T(8,128)(2,1)S(1)}, bf16[384,384]{1,0:T(8,128)(2,1)}, u32[]{:S(2)}) %copy-start.1) | copy-done | bytes 294936
  3.3 0.0 copy-start.2
  3.3 0.9 copy-done.2
  4.2 0.9 copy-done.3
  5.1 0.8 copy-done.4
  5.9 0.8 copy-done.5
  6.6 0.8 copy-done.6
  7.4 0.8 copy-done.7
  8.1 81.8 %pairformer.1 = bf16[48,24,128]{2,1,0:T(8,128)(2,1)S(1)} custom-call(bf16[48,24,128]{2,1,0:T(8,128)(2,1)S(1)} %copy-done, s32[1,384]{1,0:T(1,128)S(1)} %reshape.12.mask_ref, s32[4,4]{1,0:T(4,128)S(1)} %copy-done.8, bf16[384,384]{1,0:T(8,128)(2,1)S(1)} %copy-done.1, f32[1,128]{1,0:T(1,128)S(1)} %bitcast.5, bf16[128,512]{1,0:T(8,128)(2,1)S(1)} %copy-done.2, ...), custom_call_target="tpu_custom_call" | custom-call | tf_op jit(solution)/shard_map/pairformer/pallas_call | solution.py:400
  90.0 0.7 copy.16
  (7 shorter events, 0.0 us)
Async XLA Ops:
  0.0 0.7 copy-start.13
  0.0 0.7 copy-start.11
  0.0 0.7 copy-start.12
  0.7 0.7 copy-start.8
  0.7 0.7 copy-start.9
  0.7 0.7 copy-start.10
  1.4 1.0 %copy-start = (bf16[48,24,128]{2,1,0:T(8,128)(2,1)S(1)}, bf16[48,24,128]{2,1,0:T(8,128)(2,1)}, u32[]{:S(2)}) copy-start(bf16[48,24,128]{2,1,0:T(8,128)(2,1)} %x_hbm.1) | copy-start | bytes 884740
  2.3 1.0 %copy-start.1 = (bf16[384,384]{1,0:T(8,128)(2,1)S(1)}, bf16[384,384]{1,0:T(8,128)(2,1)}, u32[]{:S(2)}) copy-start(bf16[384,384]{1,0:T(8,128)(2,1)} %constant.2.clone.perm_hbm) | copy-start | bytes 884740
  3.3 0.9 copy-start.2
  4.2 0.9 copy-start.3
  5.1 0.8 copy-start.4
  5.9 0.8 copy-start.5
  6.6 0.8 copy-start.6
  7.4 0.8 copy-start.7

commit v3 on v2

--- a/solution.py
+++ b/solution.py
@@ -46,11 +46,16 @@
     return 1.0 / (1.0 + jnp.exp(-v))
 
 
+def far(dz):
+    return int(dz in FAR)
+
+
 def turned(w):
     return jnp.transpose(w.astype(F32))
 
 
 RING_STEPS = (2, 1, 3)
+NEAR, FAR = (1, 7, 2, 6), (3, 5, 4)
 Z_STEPS = (4, 3, 5, 2, 6, 1, 7)
 COL_STEPS = tuple((dz, dl) for dz in Z_STEPS for dl in (1, 0)) + ((0, 1),)
 XY_STEPS = tuple(sorted(
@@ -69,7 +74,7 @@
     perm_ref, w_in_ref, w_gate_ref, w_out1_ref, w_qkv_ref, w_gate2_ref, w_out2_ref,
     w_g, w_v, w_gate_t, w_o1_t, w_qv_t, w_k_t, w_gate2_t, w_o2_t, gains,
     r_send, r_recv, l_send, l_recv, z_send, z_recv, p_send, p_recv, x_send, x_recv,
-    bz_send, bz_recv, ba_send, ba_recv, bb_send, bb_recv, o_send, o_recv, local, fetch,
+    bz_send, bz_recv, ba_send, ba_recv, bb_send, bb_recv, o_send, o_recv, fetch,
 ):
     crop, row, col = lax.axis_index("crop"), lax.axis_index("row"), lax.axis_index("col")
     z, x_lo = col // 2, col % 2
@@ -88,6 +93,9 @@
             src_ref=src, dst_ref=dst, send_sem=send, recv_sem=recv,
             device_id={"row": r, "col": c}, device_id_type=MESH,
         )
+
+    def arrive(ref, sem):
+        pltpu.make_async_copy(ref, ref, sem).wait()
 
     def col_peer(dz, dl):
         return lax.rem(z + dz, ZS) * 2 + lax.rem(x_lo + dl, 2)
@@ -106,8 +114,8 @@
             signal(r, c)
     _, r, c = xy_peer(2, 0)
     signal(r, c)
-    far = x_at + 1 + 2 * (1 - x_at % 2)
-    r, c = place(lax.rem(far, 4), y, z)
+    other = x_at + 1 + 2 * (1 - x_at % 2)
+    r, c = place(lax.rem(other, 4), y, z)
     signal(r, c)
 
     fetched = [
@@ -130,17 +138,16 @@
 
     pl.semaphore_wait(barrier, COLS - 1 + 2 * (ROWS - 1))
 
-    def r_copy(i, dz, dl, arriving):
+    def r_copy(i, dz, dl):
         peer = col_peer(dz, dl)
-        slot = peer if arriving else col
-        return remote(x_hbm.at[OWN * peer + i], x_rows.at[i, slot], r_send.at[i, peer], r_recv.at[i, slot], row, peer)
+        return remote(x_hbm.at[OWN * peer + i], x_rows.at[i, col], r_send, r_recv.at[i], row, peer)
 
     def r_own(i):
-        return pltpu.make_async_copy(x_hbm.at[OWN * col + i], x_rows.at[i, col], local.at[i])
+        return pltpu.make_async_copy(x_hbm.at[OWN * col + i], x_rows.at[i, col], r_recv.at[i])
 
     for i in range(OWN):
         for dz, dl in COL_STEPS:
-            r_copy(i, dz, dl, False).start()
+            r_copy(i, dz, dl).start()
         r_own(i).start()
 
     for copy in fetched[1:6]:
@@ -152,7 +159,7 @@
     w_qv_t[0] = turned(w_qkv_ref[:, :C]).astype(BF16)
     w_qv_t[1] = turned(w_qkv_ref[:, 2 * C :]).astype(BF16)
     w_k_t[...] = turned(w_qkv_ref[:, C : 2 * C]).astype(BF16)
-    mask = mask_ref[...].astype(F32)
+    mask = mask_ref[...].reshape(1, N).astype(F32)
     lane = lax.broadcasted_iota(jnp.int32, (1, N), 1)
     key_mask = jnp.transpose(jnp.broadcast_to(mask, (C, N)))
     for b in range(4):
@@ -164,18 +171,15 @@
         penalty[96 * b : 96 * (b + 1), :] = jnp.where(part > 0.0, 0.0, MASKED)
     fetched[6].wait()
 
-    def l_copy(i, dx, dy, arriving):
+    def l_copy(i, dx, dy):
         peer, r, c = xy_peer(dx, dy)
-        slot = peer if arriving else g
-        return remote(send_l.at[i, peer], recv_l.at[i, slot], l_send.at[i, peer], l_recv.at[i, slot], r, c)
+        return remote(send_l.at[i, peer], recv_l.at[i, g], l_send, l_recv.at[i], r, c)
 
     def l_own(i):
-        return pltpu.make_async_copy(send_l.at[i, g], recv_l.at[i, g], local.at[i])
-
-    for i in range(OWN):
-        r_own(i).wait()
-        for dz, dl in COL_STEPS:
-            r_copy(i, dz, dl, True).wait_recv()
+        return pltpu.make_async_copy(send_l.at[i, g], recv_l.at[i, g], l_recv.at[i])
+
+    for i in range(OWN):
+        arrive(x_rows.at[i], r_recv.at[i])
         x_t = jnp.transpose(x_rows[i].astype(F32).reshape(N, C))
         xt[i] = x_t
         normed = norm_columns(x_t, gains[0]).astype(BF16)
@@ -185,26 +189,20 @@
         factors = sigmoid(dot(w_g[...], normed)) * dot(w_v[...], normed) * (mask * mine)
         send_l[i] = factors.astype(BF16).reshape(GS, 16, N)
         for dx, dy in XY_STEPS:
-            l_copy(i, dx, dy, False).start()
+            l_copy(i, dx, dy).start()
         l_own(i).start()
     for i in range(OWN):
         gate1[i] = sigmoid(dot(w_gate_t[...], an_t[i]))
-    for i in range(OWN):
-        for dz, dl in COL_STEPS:
-            r_copy(i, dz, dl, False).wait_send()
-
-    def z_copy(i, src, dst, send, recv, dz, arriving):
+
+    def z_copy(i, src, dst, send, recv, dz):
         peer = lax.rem(z + dz, ZS)
-        slot = peer if arriving else z
-        return remote(src.at[i, peer], dst.at[i, slot], send.at[i, peer], recv.at[i, slot], row, peer * 2 + x_lo)
-
-    def z_own(i, src, dst):
-        return pltpu.make_async_copy(src.at[i, z], dst.at[i, z], local.at[i])
-
-    for i in range(OWN):
-        l_own(i).wait()
-        for dx, dy in XY_STEPS:
-            l_copy(i, dx, dy, True).wait_recv()
+        return remote(src.at[i, peer], dst.at[i, z], send, recv, row, peer * 2 + x_lo)
+
+    def z_own(i, src, dst, recv):
+        return pltpu.make_async_copy(src.at[i, z], dst.at[i, z], recv)
+
+    for i in range(OWN):
+        arrive(recv_l.at[i], l_recv.at[i])
         arrived = recv_l[i].astype(F32).reshape(GS * 16, N)
         for b in range(3):
             wide_t[b, i * 256 : (i + 1) * 256, :] = arrived[:, b * 128 : (b + 1) * 128]
@@ -213,39 +211,27 @@
                 piece = wide_t[b, pl.ds(i * 256 + ch, GS, stride=16), :]
                 send_z[i, ch % 8, ch // 8, :, b * 128 : (b + 1) * 128] = piece.astype(BF16)
         for dz in Z_STEPS:
-            z_copy(i, send_z, recv_z, z_send, z_recv, dz, False).start()
-        z_own(i, send_z, recv_z).start()
-    for i in range(OWN):
-        for dx, dy in XY_STEPS:
-            l_copy(i, dx, dy, False).wait_send()
-    for i in range(OWN):
-        z_own(i, send_z, recv_z).wait()
-        for dz in Z_STEPS:
-            z_copy(i, send_z, recv_z, z_send, z_recv, dz, True).wait_recv()
+            z_copy(i, send_z, recv_z, z_send, z_recv, dz).start()
+        z_own(i, send_z, recv_z, z_recv).start()
+    arrive(recv_z, z_recv)
 
     right = dot(perm_ref[...], recv_z[:, :, 1].reshape(N, N)).astype(BF16)
     for i in range(OWN):
         left = recv_z[i, :, 0].reshape(ZS * GS, N)
         send_p[i] = dot_nt(left, right).astype(BF16).reshape(ZS, GS, N)
         for dz in Z_STEPS:
-            z_copy(i, send_p, recv_p, p_send, p_recv, dz, False).start()
-        z_own(i, send_p, recv_p).start()
-
-    def x_copy(i, dx, dy, arriving):
+            z_copy(i, send_p, recv_p, p_send, p_recv.at[i], dz).start()
+        z_own(i, send_p, recv_p, p_recv.at[i]).start()
+
+    def x_copy(i, dx, dy):
         peer, r, c = xy_peer(dx, dy)
-        slot = peer if arriving else g
-        return remote(send_x.at[i, peer], recv_x.at[i, slot], x_send.at[i, peer], x_recv.at[i, slot], r, c)
+        return remote(send_x.at[i, peer], recv_x.at[i, g], x_send, x_recv.at[i], r, c)
 
     def x_own(i):
-        return pltpu.make_async_copy(send_x.at[i, g], recv_x.at[i, g], local.at[i])
-
-    for i in range(OWN):
-        for dz in Z_STEPS:
-            z_copy(i, send_z, recv_z, z_send, z_recv, dz, False).wait_send()
-    for i in range(OWN):
-        z_own(i, send_p, recv_p).wait()
-        for dz in Z_STEPS:
-            z_copy(i, send_p, recv_p, p_send, p_recv, dz, True).wait_recv()
+        return pltpu.make_async_copy(send_x.at[i, g], recv_x.at[i, g], x_recv.at[i])
+
+    for i in range(OWN):
+        arrive(recv_p.at[i], p_recv.at[i])
         arrived = recv_p[i].astype(F32).reshape(ZS * GS, N)
         for b in range(3):
             wide_t[b, i * 128 : (i + 1) * 128, :] = arrived[:, b * 128 : (b + 1) * 128]
@@ -254,15 +240,13 @@
                 piece = wide_t[b, pl.ds(i * 128 + other, 8, stride=16), :]
                 send_x[i, other, :, b * 128 : (b + 1) * 128] = piece.astype(BF16)
         for dx, dy in XY_STEPS:
-            x_copy(i, dx, dy, False).start()
+            x_copy(i, dx, dy).start()
         x_own(i).start()
 
     b_at = y + crop * (x_at - y)
     a_at = x_at + crop * (y - x_at)
     for i in range(OWN):
-        x_own(i).wait()
-        for dx, dy in XY_STEPS:
-            x_copy(i, dx, dy, True).wait_recv()
+        arrive(recv_x.at[i], x_recv.at[i])
         product = recv_x[i].astype(F32).reshape(C, N)
         update = dot(w_o1_t[...], norm_columns(product, gains[1]).astype(BF16))
         middle = (xt[i] + gate1[i] * update).astype(BF16).astype(F32)
@@ -271,31 +255,41 @@
         an_t[i] = attend
         bias_all[b_at, a_at, z, i] = dot(w_bias_ref[...], attend).astype(BF16)
 
-    def bz_copy(dz, arriving):
-        peer = lax.rem(z + dz, ZS)
-        slot = peer if arriving else z
-        return remote(
-            bias_all.at[b_at, a_at, z], bias_all.at[b_at, a_at, slot], bz_send.at[peer], bz_recv.at[slot],
-            row, peer * 2 + x_lo,
-        )
-
-    def ring_place(a, b):
+    def ring_place(a, b, z):
         return place(a + crop * (b - a), b + crop * (a - b), z)
 
-    def ba_copy(d, arriving):
-        peer = lax.rem(a_at + d, 4)
-        slot = peer if arriving else a_at
-        r, c = ring_place(peer, b_at)
-        return remote(bias_all.at[b_at, a_at], bias_all.at[b_at, slot], ba_send.at[peer], ba_recv.at[slot], r, c)
-
-    def bb_copy(d, arriving):
-        peer = lax.rem(b_at + d, 4)
-        slot = peer if arriving else b_at
-        r, c = ring_place(a_at, peer)
-        return remote(bias_all.at[b_at], bias_all.at[slot], bb_send.at[peer], bb_recv.at[slot], r, c)
+    def bz_copy(dz):
+        ref = bias_all.at[b_at, a_at, z]
+        r, c = ring_place(a_at, b_at, lax.rem(z + dz, ZS))
+        return remote(ref, ref, bz_send, bz_recv.at[far(dz)], r, c)
+
+    def ba_copy(dz, d):
+        ref = bias_all.at[b_at, a_at, lax.rem(z + dz, ZS)]
+        r, c = ring_place(lax.rem(a_at + d, 4), b_at, z)
+        return remote(ref, ref, ba_send, ba_recv.at[far(dz)], r, c)
+
+    def bb_copy(dz, da, d):
+        ref = bias_all.at[b_at, lax.rem(a_at + da, 4), lax.rem(z + dz, ZS)]
+        r, c = ring_place(a_at, lax.rem(b_at + d, 4), z)
+        return remote(ref, ref, bb_send, bb_recv, r, c)
+
+    def pass_on(group):
+        for dz in group:
+            for d in RING_STEPS:
+                ba_copy(dz, d).start()
+        for dz in group:
+            for d in RING_STEPS:
+                bb_copy(dz, 0, d).start()
+
+    def pass_on_b(group):
+        for da in RING_STEPS:
+            for dz in group:
+                for d in RING_STEPS:
+                    bb_copy(dz, da, d).start()
 
     for dz in Z_STEPS:
-        bz_copy(dz, False).start()
+        bz_copy(dz).start()
+    pass_on((0,))
 
     scale = LOG2E / math.sqrt(WIDTH)
     head_of = lax.broadcasted_iota(jnp.int32, (C, N), 0)
@@ -311,23 +305,17 @@
             scores_ref[i, h] = dot(keys, jnp.where(inside, queries, 0.0).astype(BF16))
 
     project(0)
-    for dz in Z_STEPS:
-        bz_copy(dz, True).wait_recv()
-    for d in RING_STEPS:
-        ba_copy(d, False).start()
+    arrive(bias_all.at[0, 0, :4], bz_recv.at[0])
+    pass_on(NEAR)
+    arrive(bias_all.at[0, 0, :3], bz_recv.at[1])
+    pass_on(FAR)
     project(1)
-    for d in RING_STEPS:
-        ba_copy(d, True).wait_recv()
-    for d in RING_STEPS:
-        bb_copy(d, False).start()
+    arrive(bias_all.at[0, :3, :5], ba_recv.at[0])
+    pass_on_b((0,) + NEAR)
+    arrive(bias_all.at[0, :3, :3], ba_recv.at[1])
+    pass_on_b(FAR)
     project(2)
-    for i in range(OWN):
-        for dx, dy in XY_STEPS:
-            x_copy(i, dx, dy, False).wait_send()
-        for dz in Z_STEPS:
-            z_copy(i, send_p, recv_p, p_send, p_recv, dz, False).wait_send()
-    for d in RING_STEPS:
-        bb_copy(d, True).wait_recv()
+    arrive(bias_all.at[:3], bb_recv)
     for r in range(ROWS):
         for c in range(COLS):
             xx, yy = (r // 4) * 2 + c % 2, r % 4
@@ -343,13 +331,12 @@
             rows = slice(b * 128, (b + 1) * 128)
             bias_t[h, rows, :] = jnp.transpose(part) * LOG2E + penalty[rows, :]
 
-    def o_copy(i, dz, dl, arriving):
+    def o_copy(i, dz, dl):
         peer = col_peer(dz, dl)
-        slot = peer if arriving else col
-        return remote(send_o.at[i, peer], out_ref.at[OWN * slot + i], o_send.at[i, peer], o_recv.at[i, slot], row, peer)
+        return remote(send_o.at[i, peer], out_ref.at[OWN * col + i], o_send, o_recv, row, peer)
 
     def o_own(i):
-        return pltpu.make_async_copy(send_o.at[i, col], out_ref.at[OWN * col + i], local.at[i])
+        return pltpu.make_async_copy(send_o.at[i, col], out_ref.at[OWN * col + i], o_recv)
 
     for i in range(OWN):
         parts = []
@@ -363,21 +350,19 @@
         result = mid[i] + dot(w_o2_t[...], gated)
         send_o[i] = jnp.transpose(result).reshape(COLS, 24, C).astype(BF16)
         for dz, dl in COL_STEPS:
-            o_copy(i, dz, dl, False).start()
+            o_copy(i, dz, dl).start()
         o_own(i).start()
 
-    for dz in Z_STEPS:
-        bz_copy(dz, False).wait_send()
-    for d in RING_STEPS:
-        ba_copy(d, False).wait_send()
-        bb_copy(d, False).wait_send()
-    for i in range(OWN):
-        o_own(i).wait()
-        for dz, dl in COL_STEPS:
-            o_copy(i, dz, dl, True).wait_recv()
-    for i in range(OWN):
-        for dz, dl in COL_STEPS:
-            o_copy(i, dz, dl, False).wait_send()
+    arrive(x_rows.at[:, :15], r_send)
+    arrive(send_l.at[:, :15], l_send)
+    arrive(send_z.at[:, :7], z_send)
+    arrive(send_p.at[:, :7], p_send)
+    arrive(send_x.at[:, :15], x_send)
+    arrive(bias_all.at[0, 0, :7], bz_send)
+    arrive(bias_all.at[0, :3], ba_send)
+    arrive(bias_all.at[:3], bb_send)
+    arrive(send_o.at[:, :15], o_send)
+    arrive(out_ref, o_recv)
 
 
 def token_order():
@@ -417,17 +402,15 @@
             V((C, 3 * C), BF16), V((C, C), BF16), V((C, C), BF16),
             V((2 * C, C), BF16), V((2 * C, C), BF16), V((C, C), BF16), V((C, C), BF16),
             V((2, C, C), BF16), V((C, C), BF16), V((C, C), BF16), V((C, C), BF16), V((3, C, C), F32),
-            dma((OWN, COLS)), dma((OWN, COLS)), dma((OWN, GS)), dma((OWN, GS)), dma((OWN, ZS)), dma((OWN, ZS)),
-            dma((OWN, ZS)), dma((OWN, ZS)), dma((OWN, GS)), dma((OWN, GS)),
-            dma((ZS,)), dma((ZS,)), dma((4,)), dma((4,)), dma((4,)), dma((4,)),
-            dma((OWN, COLS)), dma((OWN, COLS)), dma((OWN,)), dma((7,)),
+            dma, dma((OWN,)), dma, dma((OWN,)), dma, dma, dma, dma((OWN,)), dma, dma((OWN,)),
+            dma, dma((2,)), dma, dma((2,)), dma, dma, dma, dma, dma((7,)),
         ],
         compiler_params=pltpu.CompilerParams(
-            collective_id=0, has_side_effects=True, vmem_limit_bytes=40 * 1024 * 1024
+            collective_id=0, has_side_effects=True, vmem_limit_bytes=63 * 1024 * 1024
         ),
         name="pairformer",
     )(
-        pair_state, token_mask.reshape(1, N), block_pattern, jnp.asarray(token_order(), BF16),
+        pair_state, token_mask, block_pattern, jnp.asarray(token_order(), BF16),
         triangle_norm.reshape(1, C), triangle_input, triangle_gate, product_norm.reshape(1, C), triangle_output,
         attend_norm.reshape(1, C), attend_inputs, attend_gate, attend_bias.T, attend_output,
     )

time: 91.2 us -> 76.4 us (0.84)
  Pallas kernels: 81.8 us -> 74.6 us
  local copies, waits for them, and re-layouts: 8.82 us -> 1.71 us
    pallas_call x1, Pallas kernels: 81.8 us -> 74.6 us  [shards(): pl.pallas_call(kernel, out_shape=jax.ShapeDtypeStruct(pair_state.shape, B...]
    unnamed x29 -> x1, local copies, waits for them, and re-layouts: 8.82 us -> 1.71 us
where the time goes in v3:
time: 76.4 us; the launch traced here: 76.3 us
  Pallas kernels  74.6 us (98%)
  local copies, waits for them, and re-layouts  1.71 us (2%)
    pallas_call x1, Pallas kernels, shards(): pl.pallas_call(kernel, out_shape=jax.ShapeDtypeStruct(pair_state.shape, B...  74.6 us
    unnamed x1, local copies, waits for them, and re-layouts  1.71 us

profile of v3, /device:TPU:2, one launch (start us, length us, event | category | flops | bytes accessed | tf_op | source)
XLA Modules:
  0.0 76.3 jit_solution(3306656449214682308)
XLA Ops:
  0.0 74.6 %pairformer.1 = bf16[48,24,128]{2,1,0:T(8,128)(2,1)} custom-call(bf16[48,24,128]{2,1,0:T(8,128)(2,1)} %x_hbm.1, s32[384]{0:T(512)} %mask_ref.1, s32[4,4]{1,0:T(4,128)} %pattern_ref.1, bf16[384,384]{1,0:T(8,128)(2,1)} %constant.2.clone.perm_hbm, f32[1,128]{1,0:T(1,128)} %bitcast.5, bf16[128,512]{1,0:T(8,128)(2,1)} %w_in_hbm.1, bf16[128,128]{1,0:T(8,128)(2,1)} %w_gate_hbm.1, ...), custom_call_target="tpu_custom_call" | custom-call | tf_op jit(solution)/shard_map/pairformer/pallas_call | solution.py:385
  74.6 1.7 %copy.16 = bf16[48,24,128]{2,1,0:T(8,128)(2,1)} copy(bf16[48,24,128]{2,1,0:T(8,128)(2,1)} %pairformer.1) | data formatting | bytes 589824

commit v4 on v3

--- a/solution.py
+++ b/solution.py
@@ -46,16 +46,11 @@
     return 1.0 / (1.0 + jnp.exp(-v))
 
 
-def far(dz):
-    return int(dz in FAR)
-
-
 def turned(w):
     return jnp.transpose(w.astype(F32))
 
 
 RING_STEPS = (2, 1, 3)
-NEAR, FAR = (1, 7, 2, 6), (3, 5, 4)
 Z_STEPS = (4, 3, 5, 2, 6, 1, 7)
 COL_STEPS = tuple((dz, dl) for dz in Z_STEPS for dl in (1, 0)) + ((0, 1),)
 XY_STEPS = tuple(sorted(
@@ -71,7 +66,7 @@
     out_ref,
     x_rows, send_l, recv_l, send_z, recv_z, send_p, recv_p, send_x, recv_x,
     bias_all, send_o, xt, gate1, mid, an_t, wide_t, bias_t, penalty, scores_ref, values_ref, gate2_ref,
-    perm_ref, w_in_ref, w_gate_ref, w_out1_ref, w_qkv_ref, w_gate2_ref, w_out2_ref,
+    x_ref, perm_ref, w_in_ref, w_gate_ref, w_out1_ref, w_qkv_ref, w_gate2_ref, w_out2_ref,
     w_g, w_v, w_gate_t, w_o1_t, w_qv_t, w_k_t, w_gate2_t, w_o2_t, gains,
     r_send, r_recv, l_send, l_recv, z_send, z_recv, p_send, p_recv, x_send, x_recv,
     bz_send, bz_recv, ba_send, ba_recv, bb_send, bb_recv, o_send, o_recv, fetch,
@@ -122,7 +117,7 @@
         pltpu.make_async_copy(src, dst, fetch.at[n])
         for n, (src, dst) in enumerate((
             (w_in_hbm, w_in_ref), (w_gate_hbm, w_gate_ref), (w_out1_hbm, w_out1_ref), (w_qkv_hbm, w_qkv_ref),
-            (w_gate2_hbm, w_gate2_ref), (w_out2_hbm, w_out2_ref), (perm_hbm, perm_ref),
+            (w_gate2_hbm, w_gate2_ref), (w_out2_hbm, w_out2_ref), (perm_hbm, perm_ref), (x_hbm, x_ref),
         ))
     ]
     for copy in fetched:
@@ -136,14 +131,15 @@
     for slot, ref in enumerate((norm1_ref, norm2_ref, norm3_ref)):
         gains[slot] = jnp.transpose(jnp.broadcast_to(ref[...], (C, C)))
 
+    fetched[7].wait()
     pl.semaphore_wait(barrier, COLS - 1 + 2 * (ROWS - 1))
 
     def r_copy(i, dz, dl):
         peer = col_peer(dz, dl)
-        return remote(x_hbm.at[OWN * peer + i], x_rows.at[i, col], r_send, r_recv.at[i], row, peer)
+        return remote(x_ref.at[OWN * peer + i], x_rows.at[i, col], r_send, r_recv.at[i], row, peer)
 
     def r_own(i):
-        return pltpu.make_async_copy(x_hbm.at[OWN * col + i], x_rows.at[i, col], r_recv.at[i])
+        return pltpu.make_async_copy(x_ref.at[OWN * col + i], x_rows.at[i, col], r_recv.at[i])
 
     for i in range(OWN):
         for dz, dl in COL_STEPS:
@@ -245,6 +241,24 @@
 
     b_at = y + crop * (x_at - y)
     a_at = x_at + crop * (y - x_at)
+    def ring_place(a, b, z):
+        return place(a + crop * (b - a), b + crop * (a - b), z)
+
+    def bz_copy(i, dz):
+        ref = bias_all.at[i, b_at, a_at, z]
+        r, c = ring_place(a_at, b_at, lax.rem(z + dz, ZS))
+        return remote(ref, ref, bz_send, bz_recv.at[i], r, c)
+
+    def ba_copy(i, d):
+        ref = bias_all.at[i, b_at, a_at]
+        r, c = ring_place(lax.rem(a_at + d, 4), b_at, z)
+        return remote(ref, ref, ba_send, ba_recv.at[i], r, c)
+
+    def bb_copy(i, da, d):
+        ref = bias_all.at[i, b_at, lax.rem(a_at + da, 4)]
+        r, c = ring_place(a_at, lax.rem(b_at + d, 4), z)
+        return remote(ref, ref, bb_send, bb_recv.at[i], r, c)
+
     for i in range(OWN):
         arrive(recv_x.at[i], x_recv.at[i])
         product = recv_x[i].astype(F32).reshape(C, N)
@@ -253,43 +267,9 @@
         mid[i] = middle
         attend = norm_columns(middle, gains[2]).astype(BF16)
         an_t[i] = attend
-        bias_all[b_at, a_at, z, i] = dot(w_bias_ref[...], attend).astype(BF16)
-
-    def ring_place(a, b, z):
-        return place(a + crop * (b - a), b + crop * (a - b), z)
-
-    def bz_copy(dz):
-        ref = bias_all.at[b_at, a_at, z]
-        r, c = ring_place(a_at, b_at, lax.rem(z + dz, ZS))
-        return remote(ref, ref, bz_send, bz_recv.at[far(dz)], r, c)
-
-    def ba_copy(dz, d):
-        ref = bias_all.at[b_at, a_at, lax.rem(z + dz, ZS)]
-        r, c = ring_place(lax.rem(a_at + d, 4), b_at, z)
-        return remote(ref, ref, ba_send, ba_recv.at[far(dz)], r, c)
-
-    def bb_copy(dz, da, d):
-        ref = bias_all.at[b_at, lax.rem(a_at + da, 4), lax.rem(z + dz, ZS)]
-        r, c = ring_place(a_at, lax.rem(b_at + d, 4), z)
-        return remote(ref, ref, bb_send, bb_recv, r, c)
-
-    def pass_on(group):
-        for dz in group:
-            for d in RING_STEPS:
-                ba_copy(dz, d).start()
-        for dz in group:
-            for d in RING_STEPS:
-                bb_copy(dz, 0, d).start()
-
-    def pass_on_b(group):
-        for da in RING_STEPS:
-            for dz in group:
-                for d in RING_STEPS:
-                    bb_copy(dz, da, d).start()
-
-    for dz in Z_STEPS:
-        bz_copy(dz).start()
-    pass_on((0,))
+        bias_all[i, b_at, a_at, z] = dot(w_bias_ref[...], attend).astype(BF16)
+        for dz in Z_STEPS:
+            bz_copy(i, dz).start()
 
     scale = LOG2E / math.sqrt(WIDTH)
     head_of = lax.broadcasted_iota(jnp.int32, (C, N), 0)
@@ -305,23 +285,26 @@
             scores_ref[i, h] = dot(keys, jnp.where(inside, queries, 0.0).astype(BF16))
 
     project(0)
-    arrive(bias_all.at[0, 0, :4], bz_recv.at[0])
-    pass_on(NEAR)
-    arrive(bias_all.at[0, 0, :3], bz_recv.at[1])
-    pass_on(FAR)
+    for i in range(OWN):
+        arrive(bias_all.at[i, 0, 0, :7], bz_recv.at[i])
+        for d in RING_STEPS:
+            ba_copy(i, d).start()
+        for d in RING_STEPS:
+            bb_copy(i, 0, d).start()
     project(1)
-    arrive(bias_all.at[0, :3, :5], ba_recv.at[0])
-    pass_on_b((0,) + NEAR)
-    arrive(bias_all.at[0, :3, :3], ba_recv.at[1])
-    pass_on_b(FAR)
+    for i in range(OWN):
+        arrive(bias_all.at[i, 0, :3], ba_recv.at[i])
+        for da in RING_STEPS:
+            for d in RING_STEPS:
+                bb_copy(i, da, d).start()
     project(2)
-    arrive(bias_all.at[:3], bb_recv)
-    for r in range(ROWS):
-        for c in range(COLS):
-            xx, yy = (r // 4) * 2 + c % 2, r % 4
-            b_of, a_of = yy + crop * (xx - yy), xx + crop * (yy - xx)
-            for i in range(OWN):
-                piece = bias_all[b_of, a_of, c // 2, i].astype(F32)
+    for i in range(OWN):
+        arrive(bias_all.at[i, :3], bb_recv.at[i])
+        for r in range(ROWS):
+            for c in range(COLS):
+                xx, yy = (r // 4) * 2 + c % 2, r % 4
+                b_of, a_of = yy + crop * (xx - yy), xx + crop * (yy - xx)
+                piece = bias_all[i, b_of, a_of, c // 2].astype(F32)
                 at = ((r * COLS + c) * OWN + i) * HEADS
                 for b in range(3):
                     wide_t[b, at : at + HEADS, :] = piece[:, b * 128 : (b + 1) * 128]
@@ -358,9 +341,9 @@
     arrive(send_z.at[:, :7], z_send)
     arrive(send_p.at[:, :7], p_send)
     arrive(send_x.at[:, :15], x_send)
-    arrive(bias_all.at[0, 0, :7], bz_send)
-    arrive(bias_all.at[0, :3], ba_send)
-    arrive(bias_all.at[:3], bb_send)
+    arrive(bias_all.at[:, 0, 0, :7], bz_send)
+    arrive(bias_all.at[:, 0, :3], ba_send)
+    arrive(bias_all.at[:, :3], bb_send)
     arrive(send_o.at[:, :15], o_send)
     arrive(out_ref, o_recv)
 
@@ -393,17 +376,17 @@
             V((OWN, ZS, 2, GS, N), BF16), V((OWN, ZS, 2, GS, N), BF16),
             V((OWN, ZS, GS, N), BF16), V((OWN, ZS, GS, N), BF16),
             V((OWN, GS, 8, N), BF16), V((OWN, GS, 8, N), BF16),
-            V((4, 4, ZS, OWN, HEADS, N), BF16),
+            V((OWN, 4, 4, ZS, HEADS, N), BF16),
             V((OWN, COLS, 24, C), BF16),
             V((OWN, C, N), F32), V((OWN, C, N), F32), V((OWN, C, N), F32), V((OWN, C, N), BF16),
             V((3, HEADS * N, 128), F32), V((HEADS, N, N), F32), V((N, N), F32),
             V((OWN, HEADS, N, N), F32), V((OWN, C, N), BF16), V((OWN, C, N), F32),
-            V((N, N), BF16), V((C, 4 * C), BF16), V((C, C), BF16), V((C, C), BF16),
+            V((48, 24, C), BF16), V((N, N), BF16), V((C, 4 * C), BF16), V((C, C), BF16), V((C, C), BF16),
             V((C, 3 * C), BF16), V((C, C), BF16), V((C, C), BF16),
             V((2 * C, C), BF16), V((2 * C, C), BF16), V((C, C), BF16), V((C, C), BF16),
             V((2, C, C), BF16), V((C, C), BF16), V((C, C), BF16), V((C, C), BF16), V((3, C, C), F32),
             dma, dma((OWN,)), dma, dma((OWN,)), dma, dma, dma, dma((OWN,)), dma, dma((OWN,)),
-            dma, dma((2,)), dma, dma((2,)), dma, dma, dma, dma, dma((7,)),
+            dma, dma((OWN,)), dma, dma((OWN,)), dma, dma((OWN,)), dma, dma, dma((8,)),
         ],
         compiler_params=pltpu.CompilerParams(
             collective_id=0, has_side_effects=True, vmem_limit_bytes=63 * 1024 * 1024

time: 76.4 us -> 73.7 us (0.965)
  Pallas kernels: 74.6 us -> 71.8 us
    pallas_call x1, Pallas kernels: 74.6 us -> 71.8 us  [shards(): pl.pallas_call(kernel, out_shape=jax.ShapeDtypeStruct(pair_state.shape, B...]
where the time goes in v4:
time: 73.7 us; the launch traced here: 73.5 us
  Pallas kernels  71.8 us (97%)
  local copies, waits for them, and re-layouts  1.71 us (2%)
    pallas_call x1, Pallas kernels, shards(): pl.pallas_call(kernel, out_shape=jax.ShapeDtypeStruct(pair_state.shape, B...  71.8 us
    unnamed x1, local copies, waits for them, and re-layouts  1.71 us

profile of v4, /device:TPU:2, one launch (start us, length us, event | category | flops | bytes accessed | tf_op | source)
XLA Modules:
  0.0 73.5 jit_solution(16050092315045695962)
XLA Ops:
  0.0 71.8 %pairformer.1 = bf16[48,24,128]{2,1,0:T(8,128)(2,1)} custom-call(bf16[48,24,128]{2,1,0:T(8,128)(2,1)} %x_hbm.1, s32[384]{0:T(512)} %mask_ref.1, s32[4,4]{1,0:T(4,128)} %pattern_ref.1, bf16[384,384]{1,0:T(8,128)(2,1)} %constant.2.clone.perm_hbm, f32[1,128]{1,0:T(1,128)} %bitcast.5, bf16[128,512]{1,0:T(8,128)(2,1)} %w_in_hbm.1, bf16[128,128]{1,0:T(8,128)(2,1)} %w_gate_hbm.1, ...), custom_call_target="tpu_custom_call" | custom-call | tf_op jit(solution)/shard_map/pairformer/pallas_call | solution.py:368
  71.8 1.7 %copy.16 = bf16[48,24,128]{2,1,0:T(8,128)(2,1)} copy(bf16[48,24,128]{2,1,0:T(8,128)(2,1)} %pairformer.1) | data formatting | bytes 589824

commit v5 on v4

--- a/solution.py
+++ b/solution.py
@@ -69,9 +69,9 @@
     x_ref, perm_ref, w_in_ref, w_gate_ref, w_out1_ref, w_qkv_ref, w_gate2_ref, w_out2_ref,
     w_g, w_v, w_gate_t, w_o1_t, w_qv_t, w_k_t, w_gate2_t, w_o2_t, gains,
     r_send, r_recv, l_send, l_recv, z_send, z_recv, p_send, p_recv, x_send, x_recv,
-    bz_send, bz_recv, ba_send, ba_recv, bb_send, bb_recv, o_send, o_recv, fetch,
+    bz_send, bz_recv, ba_send, bx_recv, by_recv, bb_send, bb_recv, o_send, o_recv, fetch,
 ):
-    crop, row, col = lax.axis_index("crop"), lax.axis_index("row"), lax.axis_index("col")
+    row, col = lax.axis_index("row"), lax.axis_index("col")
     z, x_lo = col // 2, col % 2
     x_hi, y = row // 4, row % 4
     g = row * 2 + x_lo
@@ -239,25 +239,26 @@
             x_copy(i, dx, dy).start()
         x_own(i).start()
 
-    b_at = y + crop * (x_at - y)
-    a_at = x_at + crop * (y - x_at)
-    def ring_place(a, b, z):
-        return place(a + crop * (b - a), b + crop * (a - b), z)
-
     def bz_copy(i, dz):
-        ref = bias_all.at[i, b_at, a_at, z]
-        r, c = ring_place(a_at, b_at, lax.rem(z + dz, ZS))
-        return remote(ref, ref, bz_send, bz_recv.at[i], r, c)
-
-    def ba_copy(i, d):
-        ref = bias_all.at[i, b_at, a_at]
-        r, c = ring_place(lax.rem(a_at + d, 4), b_at, z)
-        return remote(ref, ref, ba_send, ba_recv.at[i], r, c)
-
-    def bb_copy(i, da, d):
-        ref = bias_all.at[i, b_at, lax.rem(a_at + da, 4)]
-        r, c = ring_place(a_at, lax.rem(b_at + d, 4), z)
-        return remote(ref, ref, bb_send, bb_recv.at[i], r, c)
+        ref = bias_all.at[i, x_at, y, z]
+        return remote(ref, ref, bz_send, bz_recv.at[i], *place(x_at, y, lax.rem(z + dz, ZS)))
+
+    def plane_copy(ref, send, recv, dx, dy):
+        return remote(ref, ref, send, recv, *place(lax.rem(x_at + dx, 4), lax.rem(y + dy, 4), z))
+
+    def own_pieces(i):
+        ref = bias_all.at[i, x_at, y]
+        for d in RING_STEPS:
+            plane_copy(ref, ba_send, bx_recv.at[i], d, 0).start()
+            plane_copy(ref, ba_send, by_recv.at[i], 0, d).start()
+
+    def passed_pieces(i):
+        for e in RING_STEPS:
+            from_x = bias_all.at[i, lax.rem(x_at + e, 4), y, :4]
+            from_y = bias_all.at[i, x_at, lax.rem(y + e, 4), 4:]
+            for d in RING_STEPS:
+                plane_copy(from_x, bb_send, bb_recv.at[i], 0, d).start()
+                plane_copy(from_y, bb_send, bb_recv.at[i], d, 0).start()
 
     for i in range(OWN):
         arrive(recv_x.at[i], x_recv.at[i])
@@ -267,7 +268,7 @@
         mid[i] = middle
         attend = norm_columns(middle, gains[2]).astype(BF16)
         an_t[i] = attend
-        bias_all[i, b_at, a_at, z] = dot(w_bias_ref[...], attend).astype(BF16)
+        bias_all[i, x_at, y, z] = dot(w_bias_ref[...], attend).astype(BF16)
         for dz in Z_STEPS:
             bz_copy(i, dz).start()
 
@@ -287,24 +288,19 @@
     project(0)
     for i in range(OWN):
         arrive(bias_all.at[i, 0, 0, :7], bz_recv.at[i])
-        for d in RING_STEPS:
-            ba_copy(i, d).start()
-        for d in RING_STEPS:
-            bb_copy(i, 0, d).start()
+        own_pieces(i)
     project(1)
     for i in range(OWN):
-        arrive(bias_all.at[i, 0, :3], ba_recv.at[i])
-        for da in RING_STEPS:
-            for d in RING_STEPS:
-                bb_copy(i, da, d).start()
+        arrive(bias_all.at[i, 0, :3], bx_recv.at[i])
+        arrive(bias_all.at[i, 0, :3], by_recv.at[i])
+        passed_pieces(i)
     project(2)
     for i in range(OWN):
-        arrive(bias_all.at[i, :3], bb_recv.at[i])
+        arrive(bias_all.at[i, :3, :3], bb_recv.at[i])
         for r in range(ROWS):
             for c in range(COLS):
                 xx, yy = (r // 4) * 2 + c % 2, r % 4
-                b_of, a_of = yy + crop * (xx - yy), xx + crop * (yy - xx)
-                piece = bias_all[i, b_of, a_of, c // 2].astype(F32)
+                piece = bias_all[i, xx, yy, c // 2].astype(F32)
                 at = ((r * COLS + c) * OWN + i) * HEADS
                 for b in range(3):
                     wide_t[b, at : at + HEADS, :] = piece[:, b * 128 : (b + 1) * 128]
@@ -342,8 +338,8 @@
     arrive(send_p.at[:, :7], p_send)
     arrive(send_x.at[:, :15], x_send)
     arrive(bias_all.at[:, 0, 0, :7], bz_send)
-    arrive(bias_all.at[:, 0, :3], ba_send)
-    arrive(bias_all.at[:, :3], bb_send)
+    arrive(bias_all.at[:, :2, :3], ba_send)
+    arrive(bias_all.at[:, :3, :3], bb_send)
     arrive(send_o.at[:, :15], o_send)
     arrive(out_ref, o_recv)
 
@@ -386,7 +382,7 @@
             V((2 * C, C), BF16), V((2 * C, C), BF16), V((C, C), BF16), V((C, C), BF16),
             V((2, C, C), BF16), V((C, C), BF16), V((C, C), BF16), V((C, C), BF16), V((3, C, C), F32),
             dma, dma((OWN,)), dma, dma((OWN,)), dma, dma, dma, dma((OWN,)), dma, dma((OWN,)),
-            dma, dma((OWN,)), dma, dma((OWN,)), dma, dma((OWN,)), dma, dma, dma((8,)),
+            dma, dma((OWN,)), dma, dma((OWN,)), dma((OWN,)), dma, dma((OWN,)), dma, dma, dma((8,)),
         ],
         compiler_params=pltpu.CompilerParams(
             collective_id=0, has_side_effects=True, vmem_limit_bytes=63 * 1024 * 1024

time: 73.7 us -> 72.6 us (0.985)
  Pallas kernels: 71.8 us -> 70.7 us
    pallas_call x1, Pallas kernels: 71.8 us -> 70.7 us  [shards(): pl.pallas_call(kernel, out_shape=jax.ShapeDtypeStruct(pair_state.shape, B...]
where the time goes in v5:
time: 72.6 us; the launch traced here: 72.4 us
  Pallas kernels  70.7 us (97%)
  local copies, waits for them, and re-layouts  1.71 us (2%)
    pallas_call x1, Pallas kernels, shards(): pl.pallas_call(kernel, out_shape=jax.ShapeDtypeStruct(pair_state.shape, B...  70.7 us
    unnamed x1, local copies, waits for them, and re-layouts  1.71 us

profile of v5, /device:TPU:2, one launch (start us, length us, event | category | flops | bytes accessed | tf_op | source)
XLA Modules:
  0.0 72.4 jit_solution(17079944582267880748)
XLA Ops:
  0.0 70.7 %pairformer.1 = bf16[48,24,128]{2,1,0:T(8,128)(2,1)} custom-call(bf16[48,24,128]{2,1,0:T(8,128)(2,1)} %x_hbm.1, s32[384]{0:T(512)} %mask_ref.1, s32[4,4]{1,0:T(4,128)} %pattern_ref.1, bf16[384,384]{1,0:T(8,128)(2,1)} %constant.2.clone.perm_hbm, f32[1,128]{1,0:T(1,128)} %bitcast.5, bf16[128,512]{1,0:T(8,128)(2,1)} %w_in_hbm.1, bf16[128,128]{1,0:T(8,128)(2,1)} %w_gate_hbm.1, ...), custom_call_target="tpu_custom_call" | custom-call | tf_op jit(solution)/shard_map/pairformer/pallas_call | solution.py:364
  70.7 1.7 %copy.16 = bf16[48,24,128]{2,1,0:T(8,128)(2,1)} copy(bf16[48,24,128]{2,1,0:T(8,128)(2,1)} %pairformer.1) | data formatting | bytes 589824

commit v6 on v5

--- a/solution.py
+++ b/solution.py
@@ -64,11 +64,11 @@
     norm1_ref, w_in_hbm, w_gate_hbm, norm2_ref, w_out1_hbm,
     norm3_ref, w_qkv_hbm, w_gate2_hbm, w_bias_ref, w_out2_hbm,
     out_ref,
-    x_rows, send_l, recv_l, send_z, recv_z, send_p, recv_p, send_x, recv_x,
+    x_rows, send_lz, recv_lz, send_rx, recv_rx, send_rz, recv_rz, send_lx, recv_lx, send_p, recv_p, send_x, recv_x,
     bias_all, send_o, xt, gate1, mid, an_t, wide_t, bias_t, penalty, scores_ref, values_ref, gate2_ref,
     x_ref, perm_ref, w_in_ref, w_gate_ref, w_out1_ref, w_qkv_ref, w_gate2_ref, w_out2_ref,
-    w_g, w_v, w_gate_t, w_o1_t, w_qv_t, w_k_t, w_gate2_t, w_o2_t, gains,
-    r_send, r_recv, l_send, l_recv, z_send, z_recv, p_send, p_recv, x_send, x_recv,
+    w_g, w_v, w_gate_t, w_o1_t, w_qv_t, w_k_t, w_gate2_t, w_o2_t, gains, z_order,
+    r_send, r_recv, lz_send, lz_recv, rx_send, rx_recv, rz_send, rz_recv, lx_send, lx_recv, p_send, p_recv, x_send, x_recv,
     bz_send, bz_recv, ba_send, bx_recv, by_recv, bb_send, bb_recv, o_send, o_recv, fetch,
 ):
     row, col = lax.axis_index("row"), lax.axis_index("col")
@@ -125,9 +125,12 @@
 
     fetched[0].wait()
     w_t = jnp.concatenate([turned(w_in_ref[:, s * C : (s + 1) * C]) for s in range(4)], axis=0)
-    ga, va, gb, vb = (w_t[s * C : (s + 1) * C].reshape(GS, 8, C) for s in range(4))
-    w_g[...] = jnp.concatenate([ga, gb], axis=1).reshape(2 * C, C).astype(BF16)
-    w_v[...] = jnp.concatenate([va, vb], axis=1).reshape(2 * C, C).astype(BF16)
+    ga, va, gb, vb = (w_t[s * C : (s + 1) * C].astype(BF16) for s in range(4))
+    line, at = (lax.broadcasted_iota(jnp.int32, (C, C), d) for d in range(2))
+    z_first = jnp.where((line & 15) * ZS + (line >> 4) == at, 1.0, 0.0).astype(BF16)
+    z_order[...] = z_first
+    w_g[:C], w_g[C:] = dot(z_first, ga).astype(BF16), gb
+    w_v[:C], w_v[C:] = dot(z_first, va).astype(BF16), vb
     for slot, ref in enumerate((norm1_ref, norm2_ref, norm3_ref)):
         gains[slot] = jnp.transpose(jnp.broadcast_to(ref[...], (C, C)))
 
@@ -167,12 +170,20 @@
         penalty[96 * b : 96 * (b + 1), :] = jnp.where(part > 0.0, 0.0, MASKED)
     fetched[6].wait()
 
-    def l_copy(i, dx, dy):
-        peer, r, c = xy_peer(dx, dy)
-        return remote(send_l.at[i, peer], recv_l.at[i, g], l_send, l_recv.at[i], r, c)
-
-    def l_own(i):
-        return pltpu.make_async_copy(send_l.at[i, g], recv_l.at[i, g], l_recv.at[i])
+    def z_copy(i, src, dst, send, recv, dz):
+        peer = lax.rem(z + dz, ZS)
+        return remote(src.at[i, peer], dst.at[i, z], send, recv, row, peer * 2 + x_lo)
+
+    def z_exchange(i, src, dst, send, recv):
+        for dz in Z_STEPS:
+            z_copy(i, src, dst, send, recv, dz).start()
+        pltpu.make_async_copy(src.at[i, z], dst.at[i, z], recv).start()
+
+    def xy_exchange(i, src, dst, send, recv):
+        for dx, dy in XY_STEPS:
+            peer, r, c = xy_peer(dx, dy)
+            remote(src.at[i, peer], dst.at[i, g], send, recv, r, c).start()
+        pltpu.make_async_copy(src.at[i, g], dst.at[i, g], recv).start()
 
     for i in range(OWN):
         arrive(x_rows.at[i], r_recv.at[i])
@@ -183,61 +194,59 @@
         own_token = row * 48 + col * OWN + i
         mine = jnp.sum(jnp.where(lane == own_token, mask, 0.0), axis=1, keepdims=True)
         factors = sigmoid(dot(w_g[...], normed)) * dot(w_v[...], normed) * (mask * mine)
-        send_l[i] = factors.astype(BF16).reshape(GS, 16, N)
-        for dx, dy in XY_STEPS:
-            l_copy(i, dx, dy).start()
-        l_own(i).start()
+        send_lz[i] = factors[:C].astype(BF16).reshape(ZS, GS, N)
+        send_rx[i] = factors[C:].reshape(GS, ZS, N).astype(BF16)
+        z_exchange(i, send_lz, recv_lz, lz_send, lz_recv.at[i])
+        xy_exchange(i, send_rx, recv_rx, rx_send, rx_recv.at[i])
     for i in range(OWN):
         gate1[i] = sigmoid(dot(w_gate_t[...], an_t[i]))
 
-    def z_copy(i, src, dst, send, recv, dz):
-        peer = lax.rem(z + dz, ZS)
-        return remote(src.at[i, peer], dst.at[i, z], send, recv, row, peer * 2 + x_lo)
-
-    def z_own(i, src, dst, recv):
-        return pltpu.make_async_copy(src.at[i, z], dst.at[i, z], recv)
-
-    for i in range(OWN):
-        arrive(recv_l.at[i], l_recv.at[i])
-        arrived = recv_l[i].astype(F32).reshape(GS * 16, N)
+    def spread(i, half, arrived):
+        base = (2 * i + half) * C
         for b in range(3):
-            wide_t[b, i * 256 : (i + 1) * 256, :] = arrived[:, b * 128 : (b + 1) * 128]
-        for ch in range(16):
+            wide_t[b, base : base + C, :] = arrived[:, b * 128 : (b + 1) * 128]
+        return base
+
+    def right_on(i):
+        arrive(recv_rx.at[i], rx_recv.at[i])
+        base = spread(i, 0, recv_rx[i].astype(F32).reshape(C, N))
+        for to in range(ZS):
             for b in range(3):
-                piece = wide_t[b, pl.ds(i * 256 + ch, GS, stride=16), :]
-                send_z[i, ch % 8, ch // 8, :, b * 128 : (b + 1) * 128] = piece.astype(BF16)
-        for dz in Z_STEPS:
-            z_copy(i, send_z, recv_z, z_send, z_recv, dz).start()
-        z_own(i, send_z, recv_z, z_recv).start()
-    arrive(recv_z, z_recv)
-
-    right = dot(perm_ref[...], recv_z[:, :, 1].reshape(N, N)).astype(BF16)
-    for i in range(OWN):
-        left = recv_z[i, :, 0].reshape(ZS * GS, N)
+                piece = wide_t[b, pl.ds(base + to, GS, stride=ZS), :]
+                send_rz[i, to, :, b * 128 : (b + 1) * 128] = piece.astype(BF16)
+        z_exchange(i, send_rz, recv_rz, rz_send, rz_recv)
+
+    def left_on(i):
+        arrive(recv_lz.at[i], lz_recv.at[i])
+        base = spread(i, 1, recv_lz[i].astype(F32).reshape(C, N))
+        for to in range(GS):
+            for b in range(3):
+                piece = wide_t[b, pl.ds(base + to, ZS, stride=GS), :]
+                send_lx[i, to, :, b * 128 : (b + 1) * 128] = piece.astype(BF16)
+        xy_exchange(i, send_lx, recv_lx, lx_send, lx_recv.at[i])
+
+    right_on(0)
+    right_on(1)
+    left_on(0)
+    right_on(2)
+    left_on(1)
+    left_on(2)
+    arrive(recv_rz, rz_recv)
+    right = dot(perm_ref[...], recv_rz[...].reshape(N, N)).astype(BF16)
+    for i in range(OWN):
+        arrive(recv_lx.at[i], lx_recv.at[i])
+        left = dot(z_order[...], recv_lx[i].astype(F32).reshape(C, N).astype(BF16)).astype(BF16)
         send_p[i] = dot_nt(left, right).astype(BF16).reshape(ZS, GS, N)
-        for dz in Z_STEPS:
-            z_copy(i, send_p, recv_p, p_send, p_recv.at[i], dz).start()
-        z_own(i, send_p, recv_p, p_recv.at[i]).start()
-
-    def x_copy(i, dx, dy):
-        peer, r, c = xy_peer(dx, dy)
-        return remote(send_x.at[i, peer], recv_x.at[i, g], x_send, x_recv.at[i], r, c)
-
-    def x_own(i):
-        return pltpu.make_async_copy(send_x.at[i, g], recv_x.at[i, g], x_recv.at[i])
+        z_exchange(i, send_p, recv_p, p_send, p_recv.at[i])
 
     for i in range(OWN):
         arrive(recv_p.at[i], p_recv.at[i])
-        arrived = recv_p[i].astype(F32).reshape(ZS * GS, N)
-        for b in range(3):
-            wide_t[b, i * 128 : (i + 1) * 128, :] = arrived[:, b * 128 : (b + 1) * 128]
-        for other in range(GS):
+        base = spread(i, 0, recv_p[i].astype(F32).reshape(C, N))
+        for to in range(GS):
             for b in range(3):
-                piece = wide_t[b, pl.ds(i * 128 + other, 8, stride=16), :]
-                send_x[i, other, :, b * 128 : (b + 1) * 128] = piece.astype(BF16)
-        for dx, dy in XY_STEPS:
-            x_copy(i, dx, dy).start()
-        x_own(i).start()
+                piece = wide_t[b, pl.ds(base + to, ZS, stride=GS), :]
+                send_x[i, to, :, b * 128 : (b + 1) * 128] = piece.astype(BF16)
+        xy_exchange(i, send_x, recv_x, x_send, x_recv.at[i])
 
     def bz_copy(i, dz):
         ref = bias_all.at[i, x_at, y, z]
@@ -333,8 +342,10 @@
         o_own(i).start()
 
     arrive(x_rows.at[:, :15], r_send)
-    arrive(send_l.at[:, :15], l_send)
-    arrive(send_z.at[:, :7], z_send)
+    arrive(send_lz.at[:, :7], lz_send)
+    arrive(send_rx.at[:, :15], rx_send)
+    arrive(send_rz.at[:, :7], rz_send)
+    arrive(send_lx.at[:, :15], lx_send)
     arrive(send_p.at[:, :7], p_send)
     arrive(send_x.at[:, :15], x_send)
     arrive(bias_all.at[:, 0, 0, :7], bz_send)
@@ -368,8 +379,8 @@
         out_specs=hbm,
         scratch_shapes=[
             V((OWN, COLS, 24, C), BF16),
-            V((OWN, GS, 16, N), BF16), V((OWN, GS, 16, N), BF16),
-            V((OWN, ZS, 2, GS, N), BF16), V((OWN, ZS, 2, GS, N), BF16),
+            V((OWN, ZS, GS, N), BF16), V((OWN, ZS, GS, N), BF16), V((OWN, GS, ZS, N), BF16), V((OWN, GS, ZS, N), BF16),
+            V((OWN, ZS, GS, N), BF16), V((OWN, ZS, GS, N), BF16), V((OWN, GS, ZS, N), BF16), V((OWN, GS, ZS, N), BF16),
             V((OWN, ZS, GS, N), BF16), V((OWN, ZS, GS, N), BF16),
             V((OWN, GS, 8, N), BF16), V((OWN, GS, 8, N), BF16),
             V((OWN, 4, 4, ZS, HEADS, N), BF16),
@@ -380,8 +391,9 @@
             V((48, 24, C), BF16), V((N, N), BF16), V((C, 4 * C), BF16), V((C, C), BF16), V((C, C), BF16),
             V((C, 3 * C), BF16), V((C, C), BF16), V((C, C), BF16),
             V((2 * C, C), BF16), V((2 * C, C), BF16), V((C, C), BF16), V((C, C), BF16),
-            V((2, C, C), BF16), V((C, C), BF16), V((C, C), BF16), V((C, C), BF16), V((3, C, C), F32),
-            dma, dma((OWN,)), dma, dma((OWN,)), dma, dma, dma, dma((OWN,)), dma, dma((OWN,)),
+            V((2, C, C), BF16), V((C, C), BF16), V((C, C), BF16), V((C, C), BF16), V((3, C, C), F32), V((C, C), BF16),
+            dma, dma((OWN,)), dma, dma((OWN,)), dma, dma((OWN,)), dma, dma, dma, dma((OWN,)),
+            dma, dma((OWN,)), dma, dma((OWN,)),
             dma, dma((OWN,)), dma, dma((OWN,)), dma((OWN,)), dma, dma((OWN,)), dma, dma, dma((8,)),
         ],
         compiler_params=pltpu.CompilerParams(

time: 72.6 us -> 69.7 us (0.960)
  Pallas kernels: 70.7 us -> 67.8 us
    pallas_call x1, Pallas kernels: 70.7 us -> 67.8 us  [shards(): pl.pallas_call(kernel, out_shape=jax.ShapeDtypeStruct(pair_state.shape, B...]
where the time goes in v6:
time: 69.7 us; the launch traced here: 69.5 us
  Pallas kernels  67.8 us (97%)
  local copies, waits for them, and re-layouts  1.71 us (2%)
    pallas_call x1, Pallas kernels, shards(): pl.pallas_call(kernel, out_shape=jax.ShapeDtypeStruct(pair_state.shape, B...  67.8 us
    unnamed x1, local copies, waits for them, and re-layouts  1.71 us

profile of v6, /device:TPU:2, one launch (start us, length us, event | category | flops | bytes accessed | tf_op | source)
XLA Modules:
  0.0 69.5 jit_solution(527909330926916818)
XLA Ops:
  0.0 67.8 %pairformer.1 = bf16[48,24,128]{2,1,0:T(8,128)(2,1)} custom-call(bf16[48,24,128]{2,1,0:T(8,128)(2,1)} %x_hbm.1, s32[384]{0:T(512)} %mask_ref.1, s32[4,4]{1,0:T(4,128)} %pattern_ref.1, bf16[384,384]{1,0:T(8,128)(2,1)} %constant.2.clone.perm_hbm, f32[1,128]{1,0:T(1,128)} %bitcast.5, bf16[128,512]{1,0:T(8,128)(2,1)} %w_in_hbm.1, bf16[128,128]{1,0:T(8,128)(2,1)} %w_gate_hbm.1, ...), custom_call_target="tpu_custom_call" | custom-call | tf_op jit(solution)/shard_map/pairformer/pallas_call | solution.py:375
  67.8 1.7 %copy.16 = bf16[48,24,128]{2,1,0:T(8,128)(2,1)} copy(bf16[48,24,128]{2,1,0:T(8,128)(2,1)} %pairformer.1) | data formatting | bytes 589824

commit v7 on v6

--- a/solution.py
+++ b/solution.py
@@ -158,16 +158,17 @@
     w_qv_t[0] = turned(w_qkv_ref[:, :C]).astype(BF16)
     w_qv_t[1] = turned(w_qkv_ref[:, 2 * C :]).astype(BF16)
     w_k_t[...] = turned(w_qkv_ref[:, C : 2 * C]).astype(BF16)
-    mask = mask_ref[...].reshape(1, N).astype(F32)
+    length = jnp.sum(mask_ref[...].reshape(1, N).astype(F32), axis=1, keepdims=True)
     lane = lax.broadcasted_iota(jnp.int32, (1, N), 1)
+    mask = jnp.where((OWN * (lane & 127) + (lane >> 7)).astype(F32) < length, 1.0, 0.0)
     key_mask = jnp.transpose(jnp.broadcast_to(mask, (C, N)))
     for b in range(4):
         line = jnp.zeros((1, N), F32)
         for a in range(4):
-            inside = (lane >= 96 * a) & (lane < 96 * (a + 1))
-            line = line + jnp.where(inside, pattern_ref[a, b].astype(F32), 0.0)
-        part = wide(key_mask[96 * b : 96 * (b + 1)]) * line
-        penalty[96 * b : 96 * (b + 1), :] = jnp.where(part > 0.0, 0.0, MASKED)
+            line = line + jnp.where(((lane & 127) >> 5) == a, pattern_ref[a, b].astype(F32), 0.0)
+        for i in range(OWN):
+            rows = slice(i * 128 + 32 * b, i * 128 + 32 * (b + 1))
+            penalty[rows, :] = jnp.where(wide(key_mask[rows]) * line > 0.0, 0.0, MASKED)
     fetched[6].wait()
 
     def z_copy(i, src, dst, send, recv, dz):
@@ -187,12 +188,15 @@
 
     for i in range(OWN):
         arrive(x_rows.at[i], r_recv.at[i])
-        x_t = jnp.transpose(x_rows[i].astype(F32).reshape(N, C))
+        wide_t[0, i * N : (i + 1) * N, :] = x_rows[i].astype(F32).reshape(N, C)
+        x_t = jnp.concatenate(
+            [jnp.transpose(wide_t[0, pl.ds(i * N + b, 128, stride=OWN), :]) for b in range(OWN)], axis=1
+        )
         xt[i] = x_t
         normed = norm_columns(x_t, gains[0]).astype(BF16)
         an_t[i] = normed
         own_token = row * 48 + col * OWN + i
-        mine = jnp.sum(jnp.where(lane == own_token, mask, 0.0), axis=1, keepdims=True)
+        mine = jnp.where(own_token.astype(F32) < length, 1.0, 0.0)
         factors = sigmoid(dot(w_g[...], normed)) * dot(w_v[...], normed) * (mask * mine)
         send_lz[i] = factors[:C].astype(BF16).reshape(ZS, GS, N)
         send_rx[i] = factors[C:].reshape(GS, ZS, N).astype(BF16)
@@ -232,7 +236,9 @@
     left_on(1)
     left_on(2)
     arrive(recv_rz, rz_recv)
-    right = dot(perm_ref[...], recv_rz[...].reshape(N, N)).astype(BF16)
+    right = jnp.concatenate(
+        [dot(perm_ref[...], recv_rz[i].reshape(C, N)).astype(BF16) for i in range(OWN)], axis=0
+    )
     for i in range(OWN):
         arrive(recv_lx.at[i], lx_recv.at[i])
         left = dot(z_order[...], recv_lx[i].astype(F32).reshape(C, N).astype(BF16)).astype(BF16)
@@ -304,42 +310,42 @@
         arrive(bias_all.at[i, 0, :3], by_recv.at[i])
         passed_pieces(i)
     project(2)
-    for i in range(OWN):
-        arrive(bias_all.at[i, :3, :3], bb_recv.at[i])
+    def o_copy(b, dz, dl):
+        peer = col_peer(dz, dl)
+        return remote(send_o.at[b, peer], out_ref.at[b, pl.ds(OWN * col, OWN)], o_send, o_recv, row, peer)
+
+    def o_own(b):
+        return pltpu.make_async_copy(send_o.at[b, col], out_ref.at[b, pl.ds(OWN * col, OWN)], o_recv)
+
+    for b in range(OWN):
+        arrive(bias_all.at[b, :3, :3], bb_recv.at[b])
+        base = b * C * HEADS
         for r in range(ROWS):
             for c in range(COLS):
-                xx, yy = (r // 4) * 2 + c % 2, r % 4
-                piece = bias_all[i, xx, yy, c // 2].astype(F32)
-                at = ((r * COLS + c) * OWN + i) * HEADS
-                for b in range(3):
-                    wide_t[b, at : at + HEADS, :] = piece[:, b * 128 : (b + 1) * 128]
-    for h in range(HEADS):
-        for b in range(3):
-            part = wide_t[b, pl.ds(h, N, stride=HEADS), :]
-            rows = slice(b * 128, (b + 1) * 128)
-            bias_t[h, rows, :] = jnp.transpose(part) * LOG2E + penalty[rows, :]
-
-    def o_copy(i, dz, dl):
-        peer = col_peer(dz, dl)
-        return remote(send_o.at[i, peer], out_ref.at[OWN * col + i], o_send, o_recv, row, peer)
-
-    def o_own(i):
-        return pltpu.make_async_copy(send_o.at[i, col], out_ref.at[OWN * col + i], o_recv)
-
-    for i in range(OWN):
-        parts = []
+                piece = bias_all[b, (r // 4) * 2 + c % 2, r % 4, c // 2].astype(F32)
+                at = base + (r * COLS + c) * HEADS
+                for k in range(3):
+                    wide_t[k, at : at + HEADS, :] = piece[:, k * 128 : (k + 1) * 128]
+        lanes = slice(b * 128, (b + 1) * 128)
         for h in range(HEADS):
-            scores = scores_ref[i, h] + bias_t[h]
-            weights = jnp.exp2(scores - jnp.max(scores, axis=0, keepdims=True))
-            total = jnp.sum(weights, axis=0, keepdims=True)
-            mixed = dot(values_ref[i, WIDTH * h : WIDTH * (h + 1)], weights.astype(BF16))
-            parts.append(mixed / total)
-        gated = (gate2_ref[i] * jnp.concatenate(parts, axis=0)).astype(BF16)
-        result = mid[i] + dot(w_o2_t[...], gated)
-        send_o[i] = jnp.transpose(result).reshape(COLS, 24, C).astype(BF16)
+            for k in range(3):
+                part = wide_t[k, pl.ds(base + h, C, stride=HEADS), :]
+                rows = slice(k * 128, (k + 1) * 128)
+                bias_t[h, rows, :] = jnp.transpose(part) * LOG2E + penalty[rows, lanes]
+        for i in range(OWN):
+            parts = []
+            for h in range(HEADS):
+                scores = scores_ref[i, h, :, lanes] + bias_t[h]
+                weights = jnp.exp2(scores - jnp.max(scores, axis=0, keepdims=True))
+                total = jnp.sum(weights, axis=0, keepdims=True)
+                mixed = dot(values_ref[i, WIDTH * h : WIDTH * (h + 1)], weights.astype(BF16))
+                parts.append(mixed / total)
+            gated = (gate2_ref[i, :, lanes] * jnp.concatenate(parts, axis=0)).astype(BF16)
+            result = mid[i, :, lanes] + dot(w_o2_t[...], gated)
+            send_o[b, :, i] = jnp.transpose(result).reshape(COLS, 8, C).astype(BF16)
         for dz, dl in COL_STEPS:
-            o_copy(i, dz, dl).start()
-        o_own(i).start()
+            o_copy(b, dz, dl).start()
+        o_own(b).start()
 
     arrive(x_rows.at[:, :15], r_send)
     arrive(send_lz.at[:, :7], lz_send)
@@ -355,11 +361,17 @@
     arrive(out_ref, o_recv)
 
 
-def token_order():
-    perm = np.zeros((N, N), np.float32)
-    for t in range(N):
-        r, c, i = t // 48, (t % 48) // 3, t % 3
-        perm[t, i * ZS * GS + (c // 2) * GS + 2 * r + c % 2] = 1.0
+def interleave(blocks_ref, out_ref, lines):
+    for b in range(OWN):
+        lines[pl.ds(b, N, stride=OWN), :] = blocks_ref[b].astype(F32).reshape(N, C)
+    out_ref[...] = lines[...].reshape(out_ref.shape).astype(BF16)
+
+
+def owner_order():
+    perm = np.zeros((C, C), np.float32)
+    for owner in range(C):
+        r, c = owner // COLS, owner % COLS
+        perm[owner, (c // 2) * GS + 2 * r + c % 2] = 1.0
     return perm
 
 
@@ -372,9 +384,9 @@
     smem = pl.BlockSpec(memory_space=pltpu.SMEM)
     dma = pltpu.SemaphoreType.DMA
     V = pltpu.VMEM
-    return pl.pallas_call(
+    blocks = pl.pallas_call(
         kernel,
-        out_shape=jax.ShapeDtypeStruct(pair_state.shape, BF16),
+        out_shape=jax.ShapeDtypeStruct((OWN, 48, 8, C), BF16),
         in_specs=[hbm, vmem, smem, hbm, vmem, hbm, hbm, vmem, hbm, vmem, hbm, hbm, vmem, hbm],
         out_specs=hbm,
         scratch_shapes=[
@@ -384,11 +396,11 @@
             V((OWN, ZS, GS, N), BF16), V((OWN, ZS, GS, N), BF16),
             V((OWN, GS, 8, N), BF16), V((OWN, GS, 8, N), BF16),
             V((OWN, 4, 4, ZS, HEADS, N), BF16),
-            V((OWN, COLS, 24, C), BF16),
+            V((OWN, COLS, OWN, 8, C), BF16),
             V((OWN, C, N), F32), V((OWN, C, N), F32), V((OWN, C, N), F32), V((OWN, C, N), BF16),
-            V((3, HEADS * N, 128), F32), V((HEADS, N, N), F32), V((N, N), F32),
+            V((3, HEADS * N, 128), F32), V((HEADS, N, C), F32), V((N, N), F32),
             V((OWN, HEADS, N, N), F32), V((OWN, C, N), BF16), V((OWN, C, N), F32),
-            V((48, 24, C), BF16), V((N, N), BF16), V((C, 4 * C), BF16), V((C, C), BF16), V((C, C), BF16),
+            V((48, 24, C), BF16), V((C, C), BF16), V((C, 4 * C), BF16), V((C, C), BF16), V((C, C), BF16),
             V((C, 3 * C), BF16), V((C, C), BF16), V((C, C), BF16),
             V((2 * C, C), BF16), V((2 * C, C), BF16), V((C, C), BF16), V((C, C), BF16),
             V((2, C, C), BF16), V((C, C), BF16), V((C, C), BF16), V((C, C), BF16), V((3, C, C), F32), V((C, C), BF16),
@@ -401,10 +413,18 @@
         ),
         name="pairformer",
     )(
-        pair_state, token_mask, block_pattern, jnp.asarray(token_order(), BF16),
+        pair_state, token_mask, block_pattern, jnp.asarray(owner_order(), BF16),
         triangle_norm.reshape(1, C), triangle_input, triangle_gate, product_norm.reshape(1, C), triangle_output,
         attend_norm.reshape(1, C), attend_inputs, attend_gate, attend_bias.T, attend_output,
     )
+    return pl.pallas_call(
+        interleave,
+        out_shape=jax.ShapeDtypeStruct(pair_state.shape, BF16),
+        in_specs=[vmem],
+        out_specs=vmem,
+        scratch_shapes=[V((48 * 24, C), F32)],
+        name="interleave",
+    )(blocks)
 
 
 def solution(mesh):

time: 69.7 us -> 67.7 us (0.971)
  local copies, waits for them, and re-layouts: 1.71 us -> 0 us
    unnamed x1 -> x0, local copies, waits for them, and re-layouts: 1.71 us -> none
    pallas_call x1 -> x2, Pallas kernels: 67.8 us -> 67.6 us  [the longest x1 65.8 us: shards(): pl.pallas_call(kernel, out_shape=jax.ShapeDtypeStruct((OWN, 48, 8, C), BF...]
where the time goes in v7:
time: 67.7 us; the launch traced here: 67.6 us
  Pallas kernels  67.6 us (100%)
    pallas_call x1, Pallas kernels, shards(): pl.pallas_call(kernel, out_shape=jax.ShapeDtypeStruct((OWN, 48, 8, C), BF...  65.8 us
    pallas_call x1, Pallas kernels, shards(): pl.pallas_call(interleave, out_shape=jax.ShapeDtypeStruct(pair_state.shap...  1.74 us

profile of v7, /device:TPU:2, one launch (start us, length us, event | category | flops | bytes accessed | tf_op | source)
XLA Modules:
  0.0 67.6 jit_solution(15391239060878454841)
XLA Ops:
  0.0 65.8 %pairformer.1.blocks_ref = bf16[3,48,8,128]{3,2,1,0:T(8,128)(2,1)} custom-call(bf16[48,24,128]{2,1,0:T(8,128)(2,1)} %x_hbm.1, s32[384]{0:T(512)} %mask_ref.1, s32[4,4]{1,0:T(4,128)} %pattern_ref.1, bf16[128,128]{1,0:T(8,128)(2,1)} %constant.2.clone.perm_hbm, f32[1,128]{1,0:T(1,128)} %bitcast.5, bf16[128,512]{1,0:T(8,128)(2,1)} %w_in_hbm.1, ...), custom_call_target="tpu_custom_call" | custom-call | tf_op jit(solution)/shard_map/pairformer/pallas_call | solution.py:387
  65.8 1.7 %interleave.1 = bf16[48,24,128]{2,1,0:T(8,128)(2,1)} custom-call(bf16[3,48,8,128]{3,2,1,0:T(8,128)(2,1)} %pairformer.1.blocks_ref), custom_call_target="tpu_custom_call" | custom-call | tf_op jit(solution)/shard_map/interleave/pallas_call | solution.py:420

commit v8 on v7

--- a/solution.py
+++ b/solution.py
@@ -60,12 +60,13 @@
 
 
 def kernel(
-    x_hbm, mask_ref, pattern_ref, perm_hbm,
-    norm1_ref, w_in_hbm, w_gate_hbm, norm2_ref, w_out1_hbm,
-    norm3_ref, w_qkv_hbm, w_gate2_hbm, w_bias_ref, w_out2_hbm,
+    x_hbm, mask_hbm, pattern_hbm, perm_hbm,
+    norm1_hbm, w_in_hbm, w_gate_hbm, norm2_hbm, w_out1_hbm,
+    norm3_hbm, w_qkv_hbm, w_gate2_hbm, w_bias_hbm, w_out2_hbm,
     out_ref,
     x_rows, send_lz, recv_lz, send_rx, recv_rx, send_rz, recv_rz, send_lx, recv_lx, send_p, recv_p, send_x, recv_x,
     bias_all, send_o, xt, gate1, mid, an_t, wide_t, bias_t, penalty, scores_ref, values_ref, gate2_ref,
+    mask_ref, pattern_ref, norms_ref, w_bias_ref,
     x_ref, perm_ref, w_in_ref, w_gate_ref, w_out1_ref, w_qkv_ref, w_gate2_ref, w_out2_ref,
     w_g, w_v, w_gate_t, w_o1_t, w_qv_t, w_k_t, w_gate2_t, w_o2_t, gains, z_order,
     r_send, r_recv, lz_send, lz_recv, rx_send, rx_recv, rz_send, rz_recv, lx_send, lx_recv, p_send, p_recv, x_send, x_recv,
@@ -118,6 +119,8 @@
         for n, (src, dst) in enumerate((
             (w_in_hbm, w_in_ref), (w_gate_hbm, w_gate_ref), (w_out1_hbm, w_out1_ref), (w_qkv_hbm, w_qkv_ref),
             (w_gate2_hbm, w_gate2_ref), (w_out2_hbm, w_out2_ref), (perm_hbm, perm_ref), (x_hbm, x_ref),
+            (norm1_hbm, norms_ref.at[0]), (norm2_hbm, norms_ref.at[1]), (norm3_hbm, norms_ref.at[2]),
+            (mask_hbm, mask_ref), (pattern_hbm, pattern_ref), (w_bias_hbm, w_bias_ref),
         ))
     ]
     for copy in fetched:
@@ -131,8 +134,9 @@
     z_order[...] = z_first
     w_g[:C], w_g[C:] = dot(z_first, ga).astype(BF16), gb
     w_v[:C], w_v[C:] = dot(z_first, va).astype(BF16), vb
-    for slot, ref in enumerate((norm1_ref, norm2_ref, norm3_ref)):
-        gains[slot] = jnp.transpose(jnp.broadcast_to(ref[...], (C, C)))
+    for slot in range(3):
+        fetched[8 + slot].wait()
+        gains[slot] = jnp.transpose(jnp.broadcast_to(norms_ref[slot], (C, C)))
 
     fetched[7].wait()
     pl.semaphore_wait(barrier, COLS - 1 + 2 * (ROWS - 1))
@@ -149,7 +153,7 @@
             r_copy(i, dz, dl).start()
         r_own(i).start()
 
-    for copy in fetched[1:6]:
+    for copy in fetched[1:6] + fetched[11:]:
         copy.wait()
     w_gate_t[...] = turned(w_gate_ref[...]).astype(BF16)
     w_o1_t[...] = turned(w_out1_ref[...]).astype(BF16)
@@ -275,18 +279,6 @@
                 plane_copy(from_x, bb_send, bb_recv.at[i], 0, d).start()
                 plane_copy(from_y, bb_send, bb_recv.at[i], d, 0).start()
 
-    for i in range(OWN):
-        arrive(recv_x.at[i], x_recv.at[i])
-        product = recv_x[i].astype(F32).reshape(C, N)
-        update = dot(w_o1_t[...], norm_columns(product, gains[1]).astype(BF16))
-        middle = (xt[i] + gate1[i] * update).astype(BF16).astype(F32)
-        mid[i] = middle
-        attend = norm_columns(middle, gains[2]).astype(BF16)
-        an_t[i] = attend
-        bias_all[i, x_at, y, z] = dot(w_bias_ref[...], attend).astype(BF16)
-        for dz in Z_STEPS:
-            bz_copy(i, dz).start()
-
     scale = LOG2E / math.sqrt(WIDTH)
     head_of = lax.broadcasted_iota(jnp.int32, (C, N), 0)
 
@@ -298,18 +290,28 @@
         gate2_ref[i] = sigmoid(dot(w_gate2_t[...], attend))
         for h in range(HEADS):
             inside = (head_of >= WIDTH * h) & (head_of < WIDTH * (h + 1))
-            scores_ref[i, h] = dot(keys, jnp.where(inside, queries, 0.0).astype(BF16))
-
-    project(0)
+            scores_ref[i, h] = dot(keys, jnp.where(inside, queries, 0.0).astype(BF16)) + penalty[...]
+
+    for i in range(OWN):
+        arrive(recv_x.at[i], x_recv.at[i])
+        product = recv_x[i].astype(F32).reshape(C, N)
+        update = dot(w_o1_t[...], norm_columns(product, gains[1]).astype(BF16))
+        middle = (xt[i] + gate1[i] * update).astype(BF16).astype(F32)
+        mid[i] = middle
+        attend = norm_columns(middle, gains[2]).astype(BF16)
+        an_t[i] = attend
+        bias_all[i, x_at, y, z] = (dot(w_bias_ref[...], attend) * LOG2E).astype(BF16)
+        for dz in Z_STEPS:
+            bz_copy(i, dz).start()
+        project(i)
+
     for i in range(OWN):
         arrive(bias_all.at[i, 0, 0, :7], bz_recv.at[i])
         own_pieces(i)
-    project(1)
     for i in range(OWN):
         arrive(bias_all.at[i, 0, :3], bx_recv.at[i])
         arrive(bias_all.at[i, 0, :3], by_recv.at[i])
         passed_pieces(i)
-    project(2)
     def o_copy(b, dz, dl):
         peer = col_peer(dz, dl)
         return remote(send_o.at[b, peer], out_ref.at[b, pl.ds(OWN * col, OWN)], o_send, o_recv, row, peer)
@@ -330,8 +332,7 @@
         for h in range(HEADS):
             for k in range(3):
                 part = wide_t[k, pl.ds(base + h, C, stride=HEADS), :]
-                rows = slice(k * 128, (k + 1) * 128)
-                bias_t[h, rows, :] = jnp.transpose(part) * LOG2E + penalty[rows, lanes]
+                bias_t[h, k * 128 : (k + 1) * 128, :] = jnp.transpose(part)
         for i in range(OWN):
             parts = []
             for h in range(HEADS):
@@ -381,13 +382,12 @@
 ):
     vmem = pl.BlockSpec(memory_space=pltpu.VMEM)
     hbm = pl.BlockSpec(memory_space=pl.ANY)
-    smem = pl.BlockSpec(memory_space=pltpu.SMEM)
     dma = pltpu.SemaphoreType.DMA
     V = pltpu.VMEM
     blocks = pl.pallas_call(
         kernel,
         out_shape=jax.ShapeDtypeStruct((OWN, 48, 8, C), BF16),
-        in_specs=[hbm, vmem, smem, hbm, vmem, hbm, hbm, vmem, hbm, vmem, hbm, hbm, vmem, hbm],
+        in_specs=[hbm] * 14,
         out_specs=hbm,
         scratch_shapes=[
             V((OWN, COLS, 24, C), BF16),
@@ -400,13 +400,14 @@
             V((OWN, C, N), F32), V((OWN, C, N), F32), V((OWN, C, N), F32), V((OWN, C, N), BF16),
             V((3, HEADS * N, 128), F32), V((HEADS, N, C), F32), V((N, N), F32),
             V((OWN, HEADS, N, N), F32), V((OWN, C, N), BF16), V((OWN, C, N), F32),
+            V((N,), jnp.int32), pltpu.SMEM((4, 4), jnp.int32), V((3, 1, C), F32), V((HEADS, C), BF16),
             V((48, 24, C), BF16), V((C, C), BF16), V((C, 4 * C), BF16), V((C, C), BF16), V((C, C), BF16),
             V((C, 3 * C), BF16), V((C, C), BF16), V((C, C), BF16),
             V((2 * C, C), BF16), V((2 * C, C), BF16), V((C, C), BF16), V((C, C), BF16),
             V((2, C, C), BF16), V((C, C), BF16), V((C, C), BF16), V((C, C), BF16), V((3, C, C), F32), V((C, C), BF16),
             dma, dma((OWN,)), dma, dma((OWN,)), dma, dma((OWN,)), dma, dma, dma, dma((OWN,)),
             dma, dma((OWN,)), dma, dma((OWN,)),
-            dma, dma((OWN,)), dma, dma((OWN,)), dma((OWN,)), dma, dma((OWN,)), dma, dma, dma((8,)),
+            dma, dma((OWN,)), dma, dma((OWN,)), dma((OWN,)), dma, dma((OWN,)), dma, dma, dma((14,)),
         ],
         compiler_params=pltpu.CompilerParams(
             collective_id=0, has_side_effects=True, vmem_limit_bytes=63 * 1024 * 1024

time: 67.7 us -> 67.1 us (level)
  no operation moved by 1% of the time
where the time goes in v8:
time: 67.1 us; the launch traced here: 67 us
  Pallas kernels  67 us (100%)
    pallas_call x1, Pallas kernels, shards(): pl.pallas_call(kernel, out_shape=jax.ShapeDtypeStruct((OWN, 48, 8, C), BF...  65.3 us
    pallas_call x1, Pallas kernels, shards(): pl.pallas_call(interleave, out_shape=jax.ShapeDtypeStruct(pair_state.shap...  1.74 us

profile of v8, /device:TPU:2, one launch (start us, length us, event | category | flops | bytes accessed | tf_op | source)
XLA Modules:
  0.0 67.0 jit_solution(17562504906812879064)
XLA Ops:
  0.0 65.3 %pairformer.1.blocks_ref = bf16[3,48,8,128]{3,2,1,0:T(8,128)(2,1)} custom-call(bf16[48,24,128]{2,1,0:T(8,128)(2,1)} %x_hbm.1, s32[384]{0:T(512)} %mask_hbm.1, s32[4,4]{1,0:T(4,128)} %pattern_hbm.1, bf16[128,128]{1,0:T(8,128)(2,1)} %constant.2.clone.perm_hbm, f32[1,128]{1,0:T(1,128)} %bitcast.5, bf16[128,512]{1,0:T(8,128)(2,1)} %w_in_hbm.1, ...), custom_call_target="tpu_custom_call" | custom-call | tf_op jit(solution)/shard_map/pairformer/pallas_call | solution.py:387
  65.3 1.7 %interleave.1 = bf16[48,24,128]{2,1,0:T(8,128)(2,1)} custom-call(bf16[3,48,8,128]{3,2,1,0:T(8,128)(2,1)} %pairformer.1.blocks_ref), custom_call_target="tpu_custom_call" | custom-call | tf_op jit(solution)/shard_map/interleave/pallas_call | solution.py:421

commit v9 on v8

--- a/solution.py
+++ b/solution.py
@@ -312,12 +312,12 @@
         arrive(bias_all.at[i, 0, :3], bx_recv.at[i])
         arrive(bias_all.at[i, 0, :3], by_recv.at[i])
         passed_pieces(i)
-    def o_copy(b, dz, dl):
-        peer = col_peer(dz, dl)
-        return remote(send_o.at[b, peer], out_ref.at[b, pl.ds(OWN * col, OWN)], o_send, o_recv, row, peer)
-
-    def o_own(b):
-        return pltpu.make_async_copy(send_o.at[b, col], out_ref.at[b, pl.ds(OWN * col, OWN)], o_recv)
+    def o_exchange(b, first, count):
+        target = out_ref.at[b, pl.ds(OWN * col + first, count)]
+        for dz, dl in COL_STEPS:
+            peer = col_peer(dz, dl)
+            remote(send_o.at[b, peer, first : first + count], target, o_send, o_recv, row, peer).start()
+        pltpu.make_async_copy(send_o.at[b, col, first : first + count], target, o_recv).start()
 
     for b in range(OWN):
         arrive(bias_all.at[b, :3, :3], bb_recv.at[b])
@@ -344,9 +344,10 @@
             gated = (gate2_ref[i, :, lanes] * jnp.concatenate(parts, axis=0)).astype(BF16)
             result = mid[i, :, lanes] + dot(w_o2_t[...], gated)
             send_o[b, :, i] = jnp.transpose(result).reshape(COLS, 8, C).astype(BF16)
-        for dz, dl in COL_STEPS:
-            o_copy(b, dz, dl).start()
-        o_own(b).start()
+            if b == OWN - 1:
+                o_exchange(b, i, 1)
+        if b < OWN - 1:
+            o_exchange(b, 0, OWN)
 
     arrive(x_rows.at[:, :15], r_send)
     arrive(send_lz.at[:, :7], lz_send)
@@ -410,20 +411,21 @@
             dma, dma((OWN,)), dma, dma((OWN,)), dma((OWN,)), dma, dma((OWN,)), dma, dma, dma((14,)),
         ],
         compiler_params=pltpu.CompilerParams(
-            collective_id=0, has_side_effects=True, vmem_limit_bytes=63 * 1024 * 1024
+            collective_id=0, has_side_effects=True, vmem_limit_bytes=48 * 1024 * 1024
         ),
         name="pairformer",
-    )(
+    )(*(pltpu.with_memory_space_constraint(v, pltpu.HBM) for v in (
         pair_state, token_mask, block_pattern, jnp.asarray(owner_order(), BF16),
         triangle_norm.reshape(1, C), triangle_input, triangle_gate, product_norm.reshape(1, C), triangle_output,
         attend_norm.reshape(1, C), attend_inputs, attend_gate, attend_bias.T, attend_output,
-    )
+    )))
     return pl.pallas_call(
         interleave,
         out_shape=jax.ShapeDtypeStruct(pair_state.shape, BF16),
         in_specs=[vmem],
         out_specs=vmem,
         scratch_shapes=[V((48 * 24, C), F32)],
+        compiler_params=pltpu.CompilerParams(vmem_limit_bytes=6 * 1024 * 1024),
         name="interleave",
     )(blocks)
 

time: 67.1 us -> 66.7 us (level)
    pallas_call x1, Pallas kernels: 1.74 us -> 0.78 us  [shards(): pl.pallas_call(interleave, out_shape=jax.ShapeDtypeStruct(pair_state.shap...]
where the time goes in v9:
time: 66.7 us; the launch traced here: 66.6 us
  Pallas kernels  66.6 us (100%)
    pallas_call x1, Pallas kernels, shards(): pl.pallas_call(kernel, out_shape=jax.ShapeDtypeStruct((OWN, 48, 8, C), BF...  65.8 us

profile of v9, /device:TPU:2, one launch (start us, length us, event | category | flops | bytes accessed | tf_op | source)
XLA Modules:
  0.0 66.6 jit_solution(4261094223109126224)
XLA Ops:
  0.0 65.8 %pairformer.1.blocks_ref = bf16[3,48,8,128]{3,2,1,0:T(8,128)(2,1)S(1)} custom-call(bf16[48,24,128]{2,1,0:T(8,128)(2,1)} %x_hbm.1, s32[384]{0:T(512)} %mask_hbm.1, s32[4,4]{1,0:T(4,128)} %pattern_hbm.1, bf16[128,128]{1,0:T(8,128)(2,1)} %constant.2.clone.perm_hbm, f32[1,128]{1,0:T(1,128)} %bitcast.5, bf16[128,512]{1,0:T(8,128)(2,1)} %w_in_hbm.1, ...), custom_call_target="tpu_custom_call" | custom-call | tf_op jit(solution)/shard_map/pairformer/pallas_call | solution.py:388
  65.9 0.8 %interleave.1 = bf16[48,24,128]{2,1,0:T(8,128)(2,1)} custom-call(bf16[3,48,8,128]{3,2,1,0:T(8,128)(2,1)S(1)} %pairformer.1.blocks_ref), custom_call_target="tpu_custom_call" | custom-call | tf_op jit(solution)/shard_map/interleave/pallas_call | solution.py:422

commit v10 on v9

--- a/solution.py
+++ b/solution.py
@@ -201,13 +201,12 @@
         an_t[i] = normed
         own_token = row * 48 + col * OWN + i
         mine = jnp.where(own_token.astype(F32) < length, 1.0, 0.0)
-        factors = sigmoid(dot(w_g[...], normed)) * dot(w_v[...], normed) * (mask * mine)
-        send_lz[i] = factors[:C].astype(BF16).reshape(ZS, GS, N)
-        send_rx[i] = factors[C:].reshape(GS, ZS, N).astype(BF16)
+        factors = sigmoid(dot(w_g[C:], normed)) * dot(w_v[C:], normed) * (mask * mine)
+        send_rx[i] = factors.reshape(GS, ZS, N).astype(BF16)
+        xy_exchange(i, send_rx, recv_rx, rx_send, rx_recv.at[i])
+        factors = sigmoid(dot(w_g[:C], normed)) * dot(w_v[:C], normed) * (mask * mine)
+        send_lz[i] = factors.astype(BF16).reshape(ZS, GS, N)
         z_exchange(i, send_lz, recv_lz, lz_send, lz_recv.at[i])
-        xy_exchange(i, send_rx, recv_rx, rx_send, rx_recv.at[i])
-    for i in range(OWN):
-        gate1[i] = sigmoid(dot(w_gate_t[...], an_t[i]))
 
     def spread(i, half, arrived):
         base = (2 * i + half) * C
@@ -239,6 +238,8 @@
     right_on(2)
     left_on(1)
     left_on(2)
+    for i in range(OWN):
+        gate1[i] = sigmoid(dot(w_gate_t[...], an_t[i]))
     arrive(recv_rz, rz_recv)
     right = jnp.concatenate(
         [dot(perm_ref[...], recv_rz[i].reshape(C, N)).astype(BF16) for i in range(OWN)], axis=0
@@ -303,21 +304,24 @@
         bias_all[i, x_at, y, z] = (dot(w_bias_ref[...], attend) * LOG2E).astype(BF16)
         for dz in Z_STEPS:
             bz_copy(i, dz).start()
-        project(i)
 
     for i in range(OWN):
         arrive(bias_all.at[i, 0, 0, :7], bz_recv.at[i])
         own_pieces(i)
+        if i < OWN - 1:
+            project(i)
     for i in range(OWN):
         arrive(bias_all.at[i, 0, :3], bx_recv.at[i])
         arrive(bias_all.at[i, 0, :3], by_recv.at[i])
         passed_pieces(i)
-    def o_exchange(b, first, count):
-        target = out_ref.at[b, pl.ds(OWN * col + first, count)]
+        if i == 0:
+            project(OWN - 1)
+    def o_exchange(b):
+        target = out_ref.at[b, pl.ds(OWN * col, OWN)]
         for dz, dl in COL_STEPS:
             peer = col_peer(dz, dl)
-            remote(send_o.at[b, peer, first : first + count], target, o_send, o_recv, row, peer).start()
-        pltpu.make_async_copy(send_o.at[b, col, first : first + count], target, o_recv).start()
+            remote(send_o.at[b, peer], target, o_send, o_recv, row, peer).start()
+        pltpu.make_async_copy(send_o.at[b, col], target, o_recv).start()
 
     for b in range(OWN):
         arrive(bias_all.at[b, :3, :3], bb_recv.at[b])
@@ -344,10 +348,7 @@
             gated = (gate2_ref[i, :, lanes] * jnp.concatenate(parts, axis=0)).astype(BF16)
             result = mid[i, :, lanes] + dot(w_o2_t[...], gated)
             send_o[b, :, i] = jnp.transpose(result).reshape(COLS, 8, C).astype(BF16)
-            if b == OWN - 1:
-                o_exchange(b, i, 1)
-        if b < OWN - 1:
-            o_exchange(b, 0, OWN)
+        o_exchange(b)
 
     arrive(x_rows.at[:, :15], r_send)
     arrive(send_lz.at[:, :7], lz_send)

time: 66.7 us -> 65.5 us (0.982)
  Pallas kernels: 66.6 us -> 65.4 us
    pallas_call x1, Pallas kernels: 65.8 us -> 64.7 us  [shards(): pl.pallas_call(kernel, out_shape=jax.ShapeDtypeStruct((OWN, 48, 8, C), BF...]
where the time goes in v10:
time: 65.5 us; the launch traced here: 65.4 us
  Pallas kernels  65.4 us (100%)
    pallas_call x1, Pallas kernels, shards(): pl.pallas_call(kernel, out_shape=jax.ShapeDtypeStruct((OWN, 48, 8, C), BF...  64.7 us

profile of v10, /device:TPU:2, one launch (start us, length us, event | category | flops | bytes accessed | tf_op | source)
XLA Modules:
  0.0 65.4 jit_solution(7475079148720624544)
XLA Ops:
  0.0 64.7 %pairformer.1.blocks_ref = bf16[3,48,8,128]{3,2,1,0:T(8,128)(2,1)S(1)} custom-call(bf16[48,24,128]{2,1,0:T(8,128)(2,1)} %x_hbm.1, s32[384]{0:T(512)} %mask_hbm.1, s32[4,4]{1,0:T(4,128)} %pattern_hbm.1, bf16[128,128]{1,0:T(8,128)(2,1)} %constant.2.clone.perm_hbm, f32[1,128]{1,0:T(1,128)} %bitcast.5, bf16[128,512]{1,0:T(8,128)(2,1)} %w_in_hbm.1, ...), custom_call_target="tpu_custom_call" | custom-call | tf_op jit(solution)/shard_map/pairformer/pallas_call | solution.py:389
  64.7 0.8 %interleave.1 = bf16[48,24,128]{2,1,0:T(8,128)(2,1)} custom-call(bf16[3,48,8,128]{3,2,1,0:T(8,128)(2,1)S(1)} %pairformer.1.blocks_ref), custom_call_target="tpu_custom_call" | custom-call | tf_op jit(solution)/shard_map/interleave/pallas_call | solution.py:423

commit v11 on v10

--- a/solution.py
+++ b/solution.py
@@ -64,12 +64,12 @@
     norm1_hbm, w_in_hbm, w_gate_hbm, norm2_hbm, w_out1_hbm,
     norm3_hbm, w_qkv_hbm, w_gate2_hbm, w_bias_hbm, w_out2_hbm,
     out_ref,
-    x_rows, send_lz, recv_lz, send_rx, recv_rx, send_rz, recv_rz, send_lx, recv_lx, send_p, recv_p, send_x, recv_x,
+    x_rows, send_za, recv_za, send_fa, recv_fa, send_fb, recv_fb, send_zb, recv_zb, send_p, recv_p, send_x, recv_x,
     bias_all, send_o, xt, gate1, mid, an_t, wide_t, bias_t, penalty, scores_ref, values_ref, gate2_ref,
     mask_ref, pattern_ref, norms_ref, w_bias_ref,
     x_ref, perm_ref, w_in_ref, w_gate_ref, w_out1_ref, w_qkv_ref, w_gate2_ref, w_out2_ref,
-    w_g, w_v, w_gate_t, w_o1_t, w_qv_t, w_k_t, w_gate2_t, w_o2_t, gains, z_order,
-    r_send, r_recv, lz_send, lz_recv, rx_send, rx_recv, rz_send, rz_recv, lx_send, lx_recv, p_send, p_recv, x_send, x_recv,
+    w_g, w_v, w_gate_t, w_o1_t, w_qv_t, w_k_t, w_gate2_t, w_o2_t, gains,
+    r_send, r_recv, za_send, za_recv, fa_send, fa_recv, fb_send, fb_recv, zb_send, zb_recv, p_send, p_recv, x_send, x_recv,
     bz_send, bz_recv, ba_send, bx_recv, by_recv, bb_send, bb_recv, o_send, o_recv, fetch,
 ):
     row, col = lax.axis_index("row"), lax.axis_index("col")
@@ -131,9 +131,8 @@
     ga, va, gb, vb = (w_t[s * C : (s + 1) * C].astype(BF16) for s in range(4))
     line, at = (lax.broadcasted_iota(jnp.int32, (C, C), d) for d in range(2))
     z_first = jnp.where((line & 15) * ZS + (line >> 4) == at, 1.0, 0.0).astype(BF16)
-    z_order[...] = z_first
-    w_g[:C], w_g[C:] = dot(z_first, ga).astype(BF16), gb
-    w_v[:C], w_v[C:] = dot(z_first, va).astype(BF16), vb
+    w_g[:C], w_g[C:] = dot(z_first, gb).astype(BF16), ga
+    w_v[:C], w_v[C:] = dot(z_first, vb).astype(BF16), va
     for slot in range(3):
         fetched[8 + slot].wait()
         gains[slot] = jnp.transpose(jnp.broadcast_to(norms_ref[slot], (C, C)))
@@ -202,11 +201,11 @@
         own_token = row * 48 + col * OWN + i
         mine = jnp.where(own_token.astype(F32) < length, 1.0, 0.0)
         factors = sigmoid(dot(w_g[C:], normed)) * dot(w_v[C:], normed) * (mask * mine)
-        send_rx[i] = factors.reshape(GS, ZS, N).astype(BF16)
-        xy_exchange(i, send_rx, recv_rx, rx_send, rx_recv.at[i])
+        send_fa[i] = factors.reshape(GS, ZS, N).astype(BF16)
+        xy_exchange(i, send_fa, recv_fa, fa_send, fa_recv.at[i])
         factors = sigmoid(dot(w_g[:C], normed)) * dot(w_v[:C], normed) * (mask * mine)
-        send_lz[i] = factors.astype(BF16).reshape(ZS, GS, N)
-        z_exchange(i, send_lz, recv_lz, lz_send, lz_recv.at[i])
+        send_za[i] = factors.astype(BF16).reshape(ZS, GS, N)
+        z_exchange(i, send_za, recv_za, za_send, za_recv.at[i])
 
     def spread(i, half, arrived):
         base = (2 * i + half) * C
@@ -214,39 +213,39 @@
             wide_t[b, base : base + C, :] = arrived[:, b * 128 : (b + 1) * 128]
         return base
 
-    def right_on(i):
-        arrive(recv_rx.at[i], rx_recv.at[i])
-        base = spread(i, 0, recv_rx[i].astype(F32).reshape(C, N))
+    def plane_on(i):
+        arrive(recv_fa.at[i], fa_recv.at[i])
+        base = spread(i, 0, recv_fa[i].astype(F32).reshape(C, N))
         for to in range(ZS):
             for b in range(3):
                 piece = wide_t[b, pl.ds(base + to, GS, stride=ZS), :]
-                send_rz[i, to, :, b * 128 : (b + 1) * 128] = piece.astype(BF16)
-        z_exchange(i, send_rz, recv_rz, rz_send, rz_recv)
-
-    def left_on(i):
-        arrive(recv_lz.at[i], lz_recv.at[i])
-        base = spread(i, 1, recv_lz[i].astype(F32).reshape(C, N))
+                send_fb[i, to, :, b * 128 : (b + 1) * 128] = piece.astype(BF16)
+        z_exchange(i, send_fb, recv_fb, fb_send, fb_recv.at[i])
+
+    def z_on(i):
+        arrive(recv_za.at[i], za_recv.at[i])
+        base = spread(i, 1, recv_za[i].astype(F32).reshape(C, N))
         for to in range(GS):
             for b in range(3):
                 piece = wide_t[b, pl.ds(base + to, ZS, stride=GS), :]
-                send_lx[i, to, :, b * 128 : (b + 1) * 128] = piece.astype(BF16)
-        xy_exchange(i, send_lx, recv_lx, lx_send, lx_recv.at[i])
-
-    right_on(0)
-    right_on(1)
-    left_on(0)
-    right_on(2)
-    left_on(1)
-    left_on(2)
+                send_zb[i, to, :, b * 128 : (b + 1) * 128] = piece.astype(BF16)
+        xy_exchange(i, send_zb, recv_zb, zb_send, zb_recv)
+
+    plane_on(0)
+    plane_on(1)
+    z_on(0)
+    plane_on(2)
+    z_on(1)
+    z_on(2)
     for i in range(OWN):
         gate1[i] = sigmoid(dot(w_gate_t[...], an_t[i]))
-    arrive(recv_rz, rz_recv)
+    arrive(recv_zb, zb_recv)
     right = jnp.concatenate(
-        [dot(perm_ref[...], recv_rz[i].reshape(C, N)).astype(BF16) for i in range(OWN)], axis=0
+        [dot(perm_ref[...], recv_zb[i].astype(F32).reshape(C, N).astype(BF16)).astype(BF16) for i in range(OWN)], axis=0
     )
     for i in range(OWN):
-        arrive(recv_lx.at[i], lx_recv.at[i])
-        left = dot(z_order[...], recv_lx[i].astype(F32).reshape(C, N).astype(BF16)).astype(BF16)
+        arrive(recv_fb.at[i], fb_recv.at[i])
+        left = recv_fb[i].reshape(C, N)
         send_p[i] = dot_nt(left, right).astype(BF16).reshape(ZS, GS, N)
         z_exchange(i, send_p, recv_p, p_send, p_recv.at[i])
 
@@ -351,10 +350,10 @@
         o_exchange(b)
 
     arrive(x_rows.at[:, :15], r_send)
-    arrive(send_lz.at[:, :7], lz_send)
-    arrive(send_rx.at[:, :15], rx_send)
-    arrive(send_rz.at[:, :7], rz_send)
-    arrive(send_lx.at[:, :15], lx_send)
+    arrive(send_za.at[:, :7], za_send)
+    arrive(send_fa.at[:, :15], fa_send)
+    arrive(send_fb.at[:, :7], fb_send)
+    arrive(send_zb.at[:, :15], zb_send)
     arrive(send_p.at[:, :7], p_send)
     arrive(send_x.at[:, :15], x_send)
     arrive(bias_all.at[:, 0, 0, :7], bz_send)
@@ -374,7 +373,7 @@
     perm = np.zeros((C, C), np.float32)
     for owner in range(C):
         r, c = owner // COLS, owner % COLS
-        perm[owner, (c // 2) * GS + 2 * r + c % 2] = 1.0
+        perm[owner, (2 * r + c % 2) * ZS + c // 2] = 1.0
     return perm
 
 
@@ -406,8 +405,8 @@
             V((48, 24, C), BF16), V((C, C), BF16), V((C, 4 * C), BF16), V((C, C), BF16), V((C, C), BF16),
             V((C, 3 * C), BF16), V((C, C), BF16), V((C, C), BF16),
             V((2 * C, C), BF16), V((2 * C, C), BF16), V((C, C), BF16), V((C, C), BF16),
-            V((2, C, C), BF16), V((C, C), BF16), V((C, C), BF16), V((C, C), BF16), V((3, C, C), F32), V((C, C), BF16),
-            dma, dma((OWN,)), dma, dma((OWN,)), dma, dma((OWN,)), dma, dma, dma, dma((OWN,)),
+            V((2, C, C), BF16), V((C, C), BF16), V((C, C), BF16), V((C, C), BF16), V((3, C, C), F32),
+            dma, dma((OWN,)), dma, dma((OWN,)), dma, dma((OWN,)), dma, dma((OWN,)), dma, dma,
             dma, dma((OWN,)), dma, dma((OWN,)),
             dma, dma((OWN,)), dma, dma((OWN,)), dma((OWN,)), dma, dma((OWN,)), dma, dma, dma((14,)),
         ],

time: 65.5 us -> 63.7 us (0.973)
  Pallas kernels: 65.4 us -> 63.6 us
    pallas_call x1, Pallas kernels: 64.7 us -> 62.8 us  [shards(): pl.pallas_call(kernel, out_shape=jax.ShapeDtypeStruct((OWN, 48, 8, C), BF...]
where the time goes in v11:
time: 63.7 us; the launch traced here: 63.6 us
  Pallas kernels  63.6 us (100%)
    pallas_call x1, Pallas kernels, shards(): pl.pallas_call(kernel, out_shape=jax.ShapeDtypeStruct((OWN, 48, 8, C), BF...  62.8 us

profile of v11, /device:TPU:2, one launch (start us, length us, event | category | flops | bytes accessed | tf_op | source)
XLA Modules:
  0.0 63.6 jit_solution(4187491273581596215)
XLA Ops:
  0.0 62.8 %pairformer.1.blocks_ref = bf16[3,48,8,128]{3,2,1,0:T(8,128)(2,1)S(1)} custom-call(bf16[48,24,128]{2,1,0:T(8,128)(2,1)} %x_hbm.1, s32[384]{0:T(512)} %mask_hbm.1, s32[4,4]{1,0:T(4,128)} %pattern_hbm.1, bf16[128,128]{1,0:T(8,128)(2,1)} %constant.2.clone.perm_hbm, f32[1,128]{1,0:T(1,128)} %bitcast.5, bf16[128,512]{1,0:T(8,128)(2,1)} %w_in_hbm.1, ...), custom_call_target="tpu_custom_call" | custom-call | tf_op jit(solution)/shard_map/pairformer/pallas_call | solution.py:388
  62.8 0.8 %interleave.1 = bf16[48,24,128]{2,1,0:T(8,128)(2,1)} custom-call(bf16[3,48,8,128]{3,2,1,0:T(8,128)(2,1)S(1)} %pairformer.1.blocks_ref), custom_call_target="tpu_custom_call" | custom-call | tf_op jit(solution)/shard_map/interleave/pallas_call | solution.py:422

commit v12 on v11

--- a/solution.py
+++ b/solution.py
@@ -200,12 +200,12 @@
         an_t[i] = normed
         own_token = row * 48 + col * OWN + i
         mine = jnp.where(own_token.astype(F32) < length, 1.0, 0.0)
+        factors = sigmoid(dot(w_g[:C], normed)) * dot(w_v[:C], normed) * (mask * mine)
+        send_za[i] = factors.astype(BF16).reshape(ZS, GS, N)
+        z_exchange(i, send_za, recv_za, za_send, za_recv.at[i])
         factors = sigmoid(dot(w_g[C:], normed)) * dot(w_v[C:], normed) * (mask * mine)
         send_fa[i] = factors.reshape(GS, ZS, N).astype(BF16)
         xy_exchange(i, send_fa, recv_fa, fa_send, fa_recv.at[i])
-        factors = sigmoid(dot(w_g[:C], normed)) * dot(w_v[:C], normed) * (mask * mine)
-        send_za[i] = factors.astype(BF16).reshape(ZS, GS, N)
-        z_exchange(i, send_za, recv_za, za_send, za_recv.at[i])
 
     def spread(i, half, arrived):
         base = (2 * i + half) * C
@@ -231,12 +231,9 @@
                 send_zb[i, to, :, b * 128 : (b + 1) * 128] = piece.astype(BF16)
         xy_exchange(i, send_zb, recv_zb, zb_send, zb_recv)
 
-    plane_on(0)
-    plane_on(1)
-    z_on(0)
-    plane_on(2)
-    z_on(1)
-    z_on(2)
+    for i in range(OWN):
+        plane_on(i)
+        z_on(i)
     for i in range(OWN):
         gate1[i] = sigmoid(dot(w_gate_t[...], an_t[i]))
     arrive(recv_zb, zb_recv)
@@ -338,12 +335,15 @@
                 bias_t[h, k * 128 : (k + 1) * 128, :] = jnp.transpose(part)
         for i in range(OWN):
             parts = []
-            for h in range(HEADS):
-                scores = scores_ref[i, h, :, lanes] + bias_t[h]
-                weights = jnp.exp2(scores - jnp.max(scores, axis=0, keepdims=True))
-                total = jnp.sum(weights, axis=0, keepdims=True)
-                mixed = dot(values_ref[i, WIDTH * h : WIDTH * (h + 1)], weights.astype(BF16))
-                parts.append(mixed / total)
+            for h in range(0, HEADS, 2):
+                pair, totals = [], []
+                for k in (h, h + 1):
+                    scores = scores_ref[i, k, :, lanes] + bias_t[k]
+                    weights = jnp.exp2(scores - jnp.max(scores, axis=0, keepdims=True))
+                    totals.append(jnp.sum(weights, axis=0, keepdims=True))
+                    pair.append(weights.astype(BF16))
+                mixed = dot(values_ref[i, WIDTH * h : WIDTH * (h + 2)], jnp.concatenate(pair, axis=1))
+                parts += [mixed[:WIDTH, :C] / totals[0], mixed[WIDTH:, C:] / totals[1]]
             gated = (gate2_ref[i, :, lanes] * jnp.concatenate(parts, axis=0)).astype(BF16)
             result = mid[i, :, lanes] + dot(w_o2_t[...], gated)
             send_o[b, :, i] = jnp.transpose(result).reshape(COLS, 8, C).astype(BF16)

time: 63.7 us -> 64.1 us (level)
  no operation moved by 1% of the time
where the time goes in v12:
time: 64.1 us; the launch traced here: 64 us
  Pallas kernels  64 us (100%)
    pallas_call x1, Pallas kernels, shards(): pl.pallas_call(kernel, out_shape=jax.ShapeDtypeStruct((OWN, 48, 8, C), BF...  63.2 us

profile of v12, /device:TPU:2, one launch (start us, length us, event | category | flops | bytes accessed | tf_op | source)
XLA Modules:
  0.0 64.0 jit_solution(4124158819917204651)
XLA Ops:
  0.0 63.2 %pairformer.1.blocks_ref = bf16[3,48,8,128]{3,2,1,0:T(8,128)(2,1)S(1)} custom-call(bf16[48,24,128]{2,1,0:T(8,128)(2,1)} %x_hbm.1, s32[384]{0:T(512)} %mask_hbm.1, s32[4,4]{1,0:T(4,128)} %pattern_hbm.1, bf16[128,128]{1,0:T(8,128)(2,1)} %constant.2.clone.perm_hbm, f32[1,128]{1,0:T(1,128)} %bitcast.5, bf16[128,512]{1,0:T(8,128)(2,1)} %w_in_hbm.1, ...), custom_call_target="tpu_custom_call" | custom-call | tf_op jit(solution)/shard_map/pairformer/pallas_call | solution.py:388
  63.2 0.8 %interleave.1 = bf16[48,24,128]{2,1,0:T(8,128)(2,1)} custom-call(bf16[3,48,8,128]{3,2,1,0:T(8,128)(2,1)S(1)} %pairformer.1.blocks_ref), custom_call_target="tpu_custom_call" | custom-call | tf_op jit(solution)/shard_map/interleave/pallas_call | solution.py:422

commit v13 on v11

--- a/solution.py
+++ b/solution.py
@@ -232,10 +232,10 @@
         xy_exchange(i, send_zb, recv_zb, zb_send, zb_recv)
 
     plane_on(0)
+    z_on(0)
     plane_on(1)
-    z_on(0)
+    z_on(1)
     plane_on(2)
-    z_on(1)
     z_on(2)
     for i in range(OWN):
         gate1[i] = sigmoid(dot(w_gate_t[...], an_t[i]))

time: 63.7 us -> 63.8 us (level)
  no operation moved by 1% of the time
where the time goes in v13:
time: 63.8 us; the launch traced here: 63.7 us
  Pallas kernels  63.7 us (100%)
    pallas_call x1, Pallas kernels, shards(): pl.pallas_call(kernel, out_shape=jax.ShapeDtypeStruct((OWN, 48, 8, C), BF...  62.9 us

profile of v13, /device:TPU:2, one launch (start us, length us, event | category | flops | bytes accessed | tf_op | source)
XLA Modules:
  0.0 63.7 jit_solution(7204995885138748233)
XLA Ops:
  0.0 62.9 %pairformer.1.blocks_ref = bf16[3,48,8,128]{3,2,1,0:T(8,128)(2,1)S(1)} custom-call(bf16[48,24,128]{2,1,0:T(8,128)(2,1)} %x_hbm.1, s32[384]{0:T(512)} %mask_hbm.1, s32[4,4]{1,0:T(4,128)} %pattern_hbm.1, bf16[128,128]{1,0:T(8,128)(2,1)} %constant.2.clone.perm_hbm, f32[1,128]{1,0:T(1,128)} %bitcast.5, bf16[128,512]{1,0:T(8,128)(2,1)} %w_in_hbm.1, ...), custom_call_target="tpu_custom_call" | custom-call | tf_op jit(solution)/shard_map/pairformer/pallas_call | solution.py:388
  62.9 0.8 %interleave.1 = bf16[48,24,128]{2,1,0:T(8,128)(2,1)} custom-call(bf16[3,48,8,128]{3,2,1,0:T(8,128)(2,1)S(1)} %pairformer.1.blocks_ref), custom_call_target="tpu_custom_call" | custom-call | tf_op jit(solution)/shard_map/interleave/pallas_call | solution.py:422
